TPU v7x, 128 devices: a whole 4x4x4 slice. The times are simulated.
128 devices in a mesh: prow: 8 (over x_lo, y), pcol: 16 (over x_hi, z, core).
Axes of the slice: x: 4 (x_hi: 2, x_lo: 2; x = x_hi * 2 + x_lo), y: 4, z: 4, core: 2. Of those that a mesh axis runs over, the one named last changes fastest.
Arguments:
- window: float32 [20480, 20480], P('prow', 'pcol'), as said below
- pattern: int32 [160, 160], P('prow', 'pcol'), may hold values from 0 to 1, as said below
- row_lists: int32 [2, 2, 64], replicated, may hold values from 0 to 159, as said below
- factor: float32 [2, 20480, 256], P(None, 'prow', 'pcol'), may hold values from -0.5 to 0.5
- diag_inverse: float32 [2, 128, 256], replicated, as said below
Outputs:
- panels: float32 [2, 20480, 256], P(None, 'pcol', 'prow')
- diagonals: float32 [2, 128, 256], P(None, None, 'prow')
Inputs may be any that keep to these rules, and one draw needn't show every extreme that they name: `pattern`: Symmetric; every diagonal block is stored; about 85 in 100 blocks are stored. `row_lists`: each list names distinct blocks. The lists of level 0 never name blocks 160 - 2 and 159; list s of level 1 is the first 62 entries of list s of level 0 followed by 160 - 2 and 159. `window`: exactly symmetric. `diag_inverse`: each of the two 128 x 128 blocks of a level is symmetric up to rounding.
All inputs are finite; a program needn't handle non-finite values.
Results may differ from a plain program's by a relative error of at most 0.00011.
Values sent between devices are 32-bit elements; how exact they have to be, the bound alone decides.
A program may use at most 128 MiB of HBM per device.

v0:
```python
import jax
import jax.numpy as jnp
from jax import lax
from jax.sharding import PartitionSpec as P

BS = 128
NB = 160


exact_mode = lax.Precision.HIGHEST


def mirror_rows(row_block, col_rows):
    row_rank = lax.axis_index("prow")
    col_rank = lax.axis_index("pcol")
    own_rows = row_block.shape[0]
    offset = col_rank * col_rows - row_rank * own_rows
    inside = jnp.logical_and(offset > -col_rows, offset < own_rows).astype(jnp.float32)
    padded = jnp.pad(row_block, ((col_rows, col_rows), (0, 0)))
    start_row = jnp.clip(offset + col_rows, 0, own_rows + col_rows)
    return lax.dynamic_slice_in_dim(padded, start_row, col_rows, 0) * inside


def product_first(left_side, right_side):
    return lax.dot_general(
        left_side,
        right_side,
        (((0,), (0,)), ((), ())),
        precision=exact_mode,
        preferred_element_type=jnp.float32,
    )


def exact_dot(left_side, right_side):
    return jnp.dot(left_side, right_side, precision=exact_mode, preferred_element_type=jnp.float32)


def local(window, pattern, row_lists, factor, diag_inverse):
    row_rank = lax.axis_index("prow")
    col_rank = lax.axis_index("pcol")
    row_count = lax.axis_size("prow")
    col_count = lax.axis_size("pcol")
    local_rows, local_cols = window.shape
    row_blocks = local_rows // BS
    col_blocks = local_cols // BS
    thin_cols = factor.shape[2]
    piece_cols = 2 * BS // row_count
    block_ids = jnp.arange(NB, dtype=jnp.int32)
    row_ids = row_rank * row_blocks + jnp.arange(row_blocks, dtype=jnp.int32)
    col_ids = col_rank * col_blocks + jnp.arange(col_blocks, dtype=jnp.int32)
    keeper = (
        pattern.astype(jnp.float32)
        * (row_ids < NB - 2).astype(jnp.float32)[:, None]
        * (col_ids < NB - 2).astype(jnp.float32)[None, :]
    )
    usable = (window.reshape(row_blocks, BS, col_blocks, BS) * keeper[:, None, :, None]).reshape(
        local_rows, local_cols
    )
    col_owner = col_rank * thin_cols // BS
    row_owner = row_rank * piece_cols // BS
    within = row_rank * piece_cols - row_owner * BS
    last_row = (row_rank == row_count - 1).astype(jnp.float32)
    last_col = (col_rank == col_count - 1).astype(jnp.float32)
    slot_start = local_cols - 2 * BS
    live_list = []
    col_flag_list = []
    col_mask_list = []
    for tier_index in range(2):
        flag_table = jnp.any(
            block_ids[None, :, None] == row_lists[tier_index][:, None, :], axis=-1
        ).astype(jnp.float32)
        row_flags = lax.dynamic_slice_in_dim(flag_table, row_rank * row_blocks, row_blocks, 1)
        col_flags = lax.dynamic_slice_in_dim(flag_table, col_rank * col_blocks, col_blocks, 1)
        row_mask = jnp.repeat(jnp.where(col_owner == 0, row_flags[0], row_flags[1]), BS)
        live_list.append(factor[tier_index] * row_mask[:, None])
        col_flag_list.append(col_flags)
        col_mask_list.append(
            jnp.repeat(jnp.where(row_owner == 0, col_flags[0], col_flags[1]), BS)[:, None]
        )
    panels = []
    diagonals = []
    across = None
    diag_prev = None
    for tier_index in range(2):
        live_factor = live_list[tier_index]
        col_flags = col_flag_list[tier_index]
        col_mask = col_mask_list[tier_index]
        live_rows = lax.all_gather(live_factor, "pcol", axis=1, tiled=True)
        live_cols = lax.psum(mirror_rows(live_rows, local_cols), "prow")
        partial_value = product_first(usable, live_rows)
        if tier_index == 1:
            partial_value = partial_value + last_row * exact_dot(
                across, live_rows[local_rows - 2 * BS :]
            )
            slot_piece = lax.dynamic_slice_in_dim(
                live_cols, slot_start + row_owner * BS + within, piece_cols, 0
            )
            target = slot_start + row_owner * BS
            current = lax.dynamic_slice_in_dim(partial_value, target, BS, 0)
            added = last_col * exact_dot(diag_prev, slot_piece)
            partial_value = lax.dynamic_update_slice_in_dim(
                partial_value, current + added, target, 0
            )
        if tier_index == 0:
            reduced = lax.psum_scatter(partial_value, "prow", scatter_dimension=1, tiled=True)
            solved = -(col_mask * reduced)
            across = lax.all_gather(solved, "prow", axis=1, tiled=True)
        else:
            reduced = lax.psum_scatter(partial_value, "prow", scatter_dimension=1, tiled=True)
            live_piece = lax.dynamic_slice_in_dim(live_cols, row_rank * piece_cols, piece_cols, 1)
            inner = lax.psum(product_first(across, live_piece), "pcol")
            reduced = jnp.concatenate(
                [reduced[:slot_start], reduced[slot_start:] + last_col * inner], axis=0
            )
            solved = -(col_mask * reduced)
        owned_cols = lax.dynamic_slice_in_dim(live_cols, row_owner * BS, BS, 1)
        gram_piece = lax.psum(product_first(owned_cols, solved), "pcol")
        diag_prev = (
            lax.dynamic_slice_in_dim(diag_inverse[tier_index], row_rank * piece_cols, piece_cols, 1)
            - gram_piece
        )
        panels.append(solved)
        diagonals.append(diag_prev)
    return (jnp.stack(panels), jnp.stack(diagonals))


def solution(mesh):
    in_specs = (P("prow", "pcol"), P("prow", "pcol"), P(), P(None, "prow", "pcol"), P())
    out_specs = (P(None, "pcol", "prow"), P(None, None, "prow"))
    return jax.shard_map(local, mesh=mesh, in_specs=in_specs, out_specs=out_specs, check_vma=False)
```

profile of v0, /device:TPU:1, one launch (start us, length us, event | category | flops | bytes accessed | tf_op | source)
XLA Modules:
  0.0 464.9 jit_solution(16957370652173471739)
XLA Ops:
  7.2 0.0 all-gather.4.cloned.1.call-start
  7.2 0.7 slice_bitcast_fusion.1
  7.9 0.1 fusion.20
  8.0 0.1 fusion.21
  8.2 0.1 constant_dynamic-slice_fusion.4
  8.2 0.1 constant_dynamic-slice_fusion.2
  8.3 0.1 broadcast_bitcast_fusion.1
  8.4 0.1 broadcast_bitcast_fusion
  8.5 1.7 bitcast_multiply_fusion.4
  10.2 0.0 all-gather.4.cloned.1.call-update
  10.2 0.0 all-gather.6.cloned.1.call-start
  10.3 0.7 all-gather.6.cloned.1.call-update
  11.0 0.0 copy-start.6
  11.0 0.0 reduce-scatter.3.cloned.1.call-start
  11.0 13.9 %copy.19 = f32[2560,1280]{0,1:T(8,128)} copy(f32[2560,1280]{1,0:T(8,128)} %param.5) | data formatting | bytes 26214400 | tf_op args[0]
  25.0 0.0 copy-done.6
  25.0 0.1 multiply_multiply_fusion
  25.1 38.6 %all-gather.4.cloned.1.call-done = f32[2560,256]{0,1:T(8,128)} async-done(((f32[2560,16]{0,1:T(8,128)}), f32[2560,256]{0,1:T(8,128)}) %all-gather.4.cloned.1.call-update) | async-done | bytes 2621456 | tf_op jit(solution)/shard_map/all_gather | solution.py:88
  63.7 0.0 copy-start
  63.7 9.0 %mul.150 = f32[20,128,10,128]{1,0,3,2:T(8,128)} broadcast(f32[20,10]{0,1:T(8,128)S(1)} %multiply_multiply_fusion), dimensions={0,2} | broadcast | bytes 13108000 | tf_op jit(solution)/shard_map/mul | solution.py:56
  72.8 1.4 copy-done
  74.1 26.0 %fusion.1 = f32[1280,256]{0,1:T(8,128)} fusion(f32[2560,256]{0,1:T(8,128)} %all-gather.4.cloned.1.call-done, f32[2560,1280]{0,1:T(8,128)S(1)} %copy-done, f32[160,8,20,128]{3,2,1,0:T(8,128)} %bitcast.55), kind=kOutput, calls=%fused_computation.4 | convolution fusion | flops 10069606400 | bytes 30146560 | tf_op jit(solution)/shard_map/dot_general | solution.py:25
  100.1 0.0 reduce-scatter.3.cloned.1.call-update
  100.1 0.0 all-reduce.6.cloned.1.call-start
  100.2 2.8 fusion.3
  103.0 11.0 %all-gather.6.cloned.1.call-done = f32[2560,256]{0,1:T(8,128)} async-done(((f32[2560,16]{0,1:T(8,128)}), f32[2560,256]{0,1:T(8,128)}) %all-gather.6.cloned.1.call-update) | async-done | bytes 2621456 | tf_op jit(solution)/shard_map/all_gather | solution.py:88
  114.1 2.8 fusion.4
  116.8 0.0 copy-start.5
  116.8 0.0 copy-start.1
  116.8 0.0 all-reduce.6.cloned.1.call-update
  116.9 0.0 all-gather.8.cloned.1.call-start
  116.9 0.1 constant_dynamic-slice_fusion.3
  117.0 0.1 broadcast_bitcast_fusion.3
  117.1 33.0 %reduce-scatter.3.cloned.1.call-done = f32[1280,32]{0,1:T(8,128)} async-done(((f32[1280,256]{0,1:T(8,128)}), f32[1280,32]{0,1:T(8,128)}) %reduce-scatter.3.cloned.1.call-update) | async-done | bytes 163856 | tf_op jit(solution)/shard_map/reduce_scatter | solution.py:105
  150.1 1.6 multiply_negate_fusion
  151.7 0.0 all-gather.8.cloned.1.call-update
  151.7 0.0 reduce-scatter.5.cloned.1.call-start
  151.8 0.0 copy-done.5
  151.8 0.1 constant_dynamic-slice_fusion
  151.9 0.1 copy.22
  152.0 0.0 copy-done.1
  152.0 0.0 copy-start.2
  152.0 18.2 %fusion = f32[1280,256]{0,1:T(8,128)} fusion(f32[2560,256]{0,1:T(8,128)S(1)} %copy-done.1, f32[2560,1280]{0,1:T(8,128)} %copy.19, f32[160,8,20,128]{3,2,1,0:T(8,128)} %bitcast.56), kind=kOutput, calls=%fused_computation.3 | convolution fusion | flops 10069606400 | bytes 30146560 | tf_op jit(solution)/shard_map/dot_general | solution.py:25
  170.2 68.2 %all-reduce.6.cloned.1.call-done = (f32[1280,256]{0,1:T(8,128)}, f32[1280,256]{0,1:T(8,128)}) async-done(((f32[1280,256]{0,1:T(8,128)}, f32[1280,256]{0,1:T(8,128)}), (f32[1280,256]{0,1:T(8,128)}, f32[1280,256]{0,1:T(8,128)})) %all-reduce.6.cloned.1.call-update) | async-done | bytes 2621456 | tf_op jit(solution)/shard_map/psum | solution.py:89
  238.4 0.0 copy-done.2
  238.4 1.8 fusion.9
  240.2 37.2 %all-gather.8.cloned.1.call-done = f32[1280,256]{0,1:T(8,128)} async-done(((f32[1280,32]{0,1:T(8,128)}), f32[1280,256]{0,1:T(8,128)}) %all-gather.8.cloned.1.call-update) | async-done | bytes 1310736 | tf_op jit(solution)/shard_map/all_gather | solution.py:107
  277.4 2.5 fusion.17
  280.0 66.1 %all-reduce.2 = (f32[128,32]{0,1:T(8,128)S(1)}, f32[256,32]{0,1:T(8,128)S(1)}) all-reduce(f32[128,32]{0,1:T(8,128)S(1)} %fusion.9, f32[256,32]{0,1:T(8,128)S(1)} %fusion.17), channel_id=1, replica_groups=mesh['prow'=8,'pcol'=16] {'pcol'}, use_global_device_ids=true, to_apply=%region_4.5 | all-reduce | flops 12288 | bytes 98304 | tf_op jit(solution)/shard_map/psum | solution.py:117
  346.1 4.1 fusion.2
  350.2 2.0 fusion.6
  352.2 0.0 reduce-scatter.5.cloned.1.call-update
  352.2 0.1 constant_dynamic-slice_fusion.1
  352.3 0.1 copy.24
  352.4 0.1 broadcast_bitcast_fusion.2
  352.5 0.0 copy-done.4
  352.5 37.0 %reduce-scatter.5.cloned.1.call-done = f32[1280,32]{0,1:T(8,128)} async-done(((f32[1280,256]{0,1:T(8,128)}), f32[1280,32]{0,1:T(8,128)}) %reduce-scatter.5.cloned.1.call-update) | async-done | bytes 163856 | tf_op jit(solution)/shard_map/reduce_scatter | solution.py:109
  389.5 0.9 fusion.35
  390.4 0.8 slice_add_fusion
  391.2 0.0 copy-done.3
  391.2 0.7 fusion.7
  391.9 64.7 %psum.39 = f32[128,32]{0,1:T(8,128)S(1)} all-reduce(f32[128,32]{0,1:T(8,128)S(1)} %fusion.7), channel_id=1, replica_groups=mesh['prow'=8,'pcol'=16] {'pcol'}, use_global_device_ids=true, to_apply=%region_8.9 | all-reduce | flops 4096 | bytes 32768 | tf_op jit(solution)/shard_map/psum | solution.py:117
  456.6 0.7 pad_maximum_fusion
  457.4 0.6 pad_maximum_fusion.1
  (14 shorter events, 0.1 us)
Async XLA Ops:
  7.2 56.6 %all-gather.4.cloned.1.call-start = ((), (), s32[]{:S(2)}) async-start(), calls=%async_computation.2 | async-start | bytes 2785280 | tf_op jit(solution)/shard_map/all_gather | solution.py:88
  10.2 103.8 %all-gather.6.cloned.1.call-start = ((), (), s32[]{:S(2)}) async-start(), calls=%async_computation.4 | async-start | bytes 2785280 | tf_op jit(solution)/shard_map/all_gather | solution.py:88
  11.0 14.0 %copy-start.6 = (s32[20,10]{0,1:T(8,128)S(1)}, s32[20,10]{0,1:T(8,128)}, u32[]{:S(2)}) copy-start(s32[20,10]{0,1:T(8,128)} %param.6) | copy-start | bytes 2404
  11.0 139.1 %reduce-scatter.3.cloned.1.call-start = ((), (), s32[]{:S(2)}) async-start(), calls=%async_computation.3 | async-start | bytes 1474560 | tf_op jit(solution)/shard_map/reduce_scatter | solution.py:105
  63.7 10.4 %copy-start = (f32[2560,1280]{0,1:T(8,128)S(1)}, f32[2560,1280]{0,1:T(8,128)}, u32[]{:S(2)}) copy-start(f32[2560,1280]{0,1:T(8,128)} %copy.19) | copy-start | bytes 39321604
  100.1 138.2 %all-reduce.6.cloned.1.call-start = ((), (), s32[]{:S(2)}) async-start(), calls=%async_computation.7 | async-start | bytes 5242880 | tf_op jit(solution)/shard_map/psum | solution.py:89
  116.8 35.0 %copy-start.5 = (f32[2,128,256]{2,1,0:T(8,128)S(1)}, f32[2,128,256]{2,1,0:T(8,128)}, u32[]{:S(2)}) copy-start(f32[2,128,256]{2,1,0:T(8,128)} %param.9) | copy-start | bytes 786436
  116.8 35.2 %copy-start.1 = (f32[2560,256]{0,1:T(8,128)S(1)}, f32[2560,256]{0,1:T(8,128)}, u32[]{:S(2)}) copy-start(f32[2560,256]{0,1:T(8,128)} %all-gather.6.cloned.1.call-done) | copy-start | bytes 7864324
  116.9 160.6 %all-gather.8.cloned.1.call-start = ((), (), s32[]{:S(2)}) async-start(), calls=%async_computation.5 | async-start | bytes 1474560 | tf_op jit(solution)/shard_map/all_gather | solution.py:107
  151.7 237.8 %reduce-scatter.5.cloned.1.call-start = ((), (), s32[]{:S(2)}) async-start(), calls=%async_computation.6 | async-start | bytes 1474560 | tf_op jit(solution)/shard_map/reduce_scatter | solution.py:109
  152.0 86.4 %copy-start.2 = (f32[1280,32]{0,1:T(8,128)S(1)}, f32[1280,32]{0,1:T(8,128)}, u32[]{:S(2)}) copy-start(f32[1280,32]{0,1:T(8,128)} %multiply_negate_fusion) | copy-start | bytes 491524
  350.2 2.3 copy-start.4
  352.2 39.0 %copy-start.3 = (f32[1280,256]{0,1:T(8,128)S(1)}, f32[1280,256]{0,1:T(8,128)}, u32[]{:S(2)}) copy-start(f32[1280,256]{0,1:T(8,128)} %get-tuple-element.4) | copy-start | bytes 3932164
Sparse Core Ops, SparseCore 0:
  11.0 52.6 all-gather.3
  66.2 47.8 all-gather.5
  116.5 33.6 reduce-scatter.2
  152.5 85.8 all-reduce.5
  240.4 36.9 all-gather.7
  352.3 37.1 reduce-scatter.4
where the time goes:
time: 470 us; the launch traced here: 465 us
  waiting for transfers between devices  226 us (48%)
  blocking collectives  131 us (28%)
  matrix products  55.4 us (12%)
  local copies, waits for them, and re-layouts  26.8 us (6%)
  between operations  14.3 us (3%)
  other arithmetic  11.4 us (2%)
    psum x2, blocking collectives, local(): gram_piece = lax.psum(product_first(owned_cols, solved), 'pcol')  131 us
    reduce_scatter x2, waiting for transfers between devices, local(): lax.psum_scatter(partial_value, 'prow', scatter_dimension=1, tiled=True)  70 us
    psum x1, waiting for transfers between devices, local(): live_cols = lax.psum(mirror_rows(live_rows, local_cols), 'prow')  68.2 us
    all_gather x2, waiting for transfers between devices, local(): live_rows = lax.all_gather(live_factor, 'pcol', axis=1, tiled=True)  49.6 us
    dot_general x5, matrix products, product_first(): lax.dot_general(left_side, right_side, (((0,), (0,)), ((), ())), precisio...  49.3 us
    all_gather x1, waiting for transfers between devices, local(): across = lax.all_gather(solved, 'prow', axis=1, tiled=True)  37.2 us
    unnamed x15, local copies, waits for them, and re-layouts  15.3 us
  transfers between devices with their start and end apart: 6, of which 6 were waited for; matrix products, arithmetic and copies ran while one was open for 17% of the time, Pallas kernels for 0%

commit v1 on v0

v1 whole, which is shorter than its diff:
```python
import jax
import jax.numpy as jnp
from jax import lax
from jax.experimental import pallas as pl
from jax.experimental.pallas import tpu as pltpu
from jax.sharding import PartitionSpec as P

BS = 128
NB = 160
RB = 20
CB = 10
ROWS = RB * BS
COLS = CB * BS
SMALL = 512
LANES = 2 * COLS + SMALL
MESH = pl.DeviceIdType.MESH
F32 = jnp.float32
BF16 = jnp.bfloat16


def remote(src, dst, send, recv, device):
    return pltpu.make_async_remote_copy(
        src_ref=src, dst_ref=dst, send_sem=send, recv_sem=recv, device_id=device, device_id_type=MESH
    )


def coords():
    r = lax.axis_index("prow")
    c = lax.axis_index("pcol")
    return r, c, r // 4, r % 4, c // 8, (c // 2) % 4, c % 2


class PairRing:
    def __init__(self, send, recv, block, half, device, p, y, sent):
        self.s, self.r, self.block, self.half, self.device = send, recv, block, half, device
        self.p, self.y, self.sent = p, y, sent
        self.q = 1 - p
        self.right, self.left, self.far = (y + 1) % 4, (y + 3) % 4, (y + 2) % 4

    def push(self, k, src, dst, device):
        copy = remote(src, dst, self.s.at[k], self.r.at[k], device)
        copy.start()
        self.sent.append(copy)

    def wait(self, k, ref):
        remote(ref, ref, self.s.at[k], self.r.at[k], self.device(self.p, self.right)).wait_recv()

    def start(self, src):
        own = self.block(self.p, self.y)
        self.push(0, src, own, self.device(self.q, self.y))
        self.push(1, src, own, self.device(self.p, self.right))
        self.push(2, src, own, self.device(self.p, self.left))

    def from_left(self, own):
        k, p = (1, self.p) if own else (5, self.q)
        self.wait(k, self.block(p, self.left))
        part = self.half(p, self.left, 0)
        self.push(k + 2, part, part, self.device(self.p, self.right))

    def from_right(self, own):
        k, p = (2, self.p) if own else (6, self.q)
        self.wait(k, self.block(p, self.right))
        part = self.half(p, self.right, 1)
        self.push(k + 2, part, part, self.device(self.p, self.left))

    def from_pair(self):
        other = self.block(self.q, self.y)
        self.wait(0, other)
        self.push(5, other, other, self.device(self.p, self.right))
        self.push(6, other, other, self.device(self.p, self.left))

    def from_far(self, own):
        k, p = (3, self.p) if own else (7, self.q)
        self.wait(k, self.half(p, self.far, 0))
        self.wait(k + 1, self.half(p, self.far, 1))


def gather_kernel(f_ref, fr_ref, fc_ref, q_ref, as_, ar, bs, br, cs, cr, ts, tr, qs, qr, ks, kr, local):
    r, c, xl, y, xh, z, k = coords()
    cc = c // 2
    other = c + 1 - 2 * k
    diagonal = r == cc
    barrier = pltpu.get_barrier_semaphore()

    def greet(device):
        pl.semaphore_signal(barrier, inc=1, device_id=device, device_id_type=MESH)

    for d in range(1, 8):
        greet((r, ((cc + d) % 8) * 2 + k))
        greet(((r + d) % 8, c))
    greet((r, other))

    @pl.when(jnp.logical_not(diagonal))
    def _():
        greet((cc, 2 * r))
        greet((cc, 2 * r + 1))
        pl.semaphore_wait(barrier, 17)

    @pl.when(diagonal)
    def _():
        pl.semaphore_wait(barrier, 15)

    sent = []
    ga = PairRing(
        as_, ar,
        lambda p, w: fr_ref.at[p * 8 + w * 2 + k],
        lambda p, w, h: fr_ref.at[p * 8 + w * 2 + k, h],
        lambda p, w: (r, p * 8 + w * 2 + k),
        xh, z, sent,
    )
    gb = PairRing(
        bs, br,
        lambda p, w: fc_ref.at[p * 4 + w],
        lambda p, w, h: fc_ref.at[p * 4 + w, h],
        lambda p, w: (p * 4 + w, c),
        xl, y, sent,
    )
    last = f_ref.at[1, :, pl.ds(ROWS - 2 * BS, 2 * BS)]
    own_q = q_ref.at[cc, k]

    @pl.when(r == 7)
    def _():
        copy = pltpu.make_async_copy(last, own_q, local.at[0])
        copy.start()
        for d in range(7):
            remote(last, own_q, qs.at[d], qr.at[0], (d, c)).start()

    ga.start(f_ref)
    own = pltpu.make_async_copy(f_ref, fr_ref.at[c], local.at[1])
    own.start()

    @pl.when(jnp.logical_not(diagonal))
    def _():
        for h in range(2):
            remote(
                f_ref.at[:, :, pl.ds(h * COLS, COLS)], fc_ref.at[cc, k], ts.at[h], tr.at[k], (cc, 2 * r + h)
            ).start()

    @pl.when(diagonal)
    def _():
        remote(
            f_ref.at[:, :, pl.ds((1 - k) * COLS, COLS)], fc_ref.at[cc, k], ts.at[0], tr.at[k], (r, other)
        ).start()
        pltpu.make_async_copy(f_ref.at[:, :, pl.ds(k * COLS, COLS)], fc_ref.at[r, k], local.at[2]).start()

    def swap(chip, src=None):
        block = fr_ref.at[chip * 2 + k]
        copy = remote(block if src is None else src, block, cs.at[chip], cr.at[chip], (r, other))
        copy.start()
        sent.append(copy)

    swap(cc, f_ref)

    @pl.when(r == 7)
    def _():
        pltpu.make_async_copy(last, own_q, local.at[0]).wait()

    @pl.when(r != 7)
    def _():
        remote(own_q, own_q, qs.at[0], qr.at[0], (r, other)).wait_recv()

    for d in range(1, 8):
        copy = remote(own_q, own_q, qs.at[7 + d], qr.at[d], (r, ((cc + d) % 8) * 2 + k))
        copy.start()
        sent.append(copy)

    chip = lambda p, w: p * 4 + w
    right, left, far = (z + 1) % 4, (z + 3) % 4, (z + 2) % 4
    mine = fc_ref.at[r]

    @pl.when(jnp.logical_not(diagonal))
    def _():
        for h in range(2):
            part = fc_ref.at[r, h]
            remote(part, part, ts.at[h], tr.at[h], (r, other)).wait_recv()

    @pl.when(diagonal)
    def _():
        part = fc_ref.at[r, 1 - k]
        remote(part, part, ts.at[0], tr.at[1 - k], (r, other)).wait_recv()
        pltpu.make_async_copy(f_ref.at[:, :, pl.ds(k * COLS, COLS)], fc_ref.at[r, k], local.at[2]).wait()

    gb.start(mine)
    ga.from_left(True)
    swap(chip(xh, left))
    ga.from_right(True)
    swap(chip(xh, right))
    ga.from_pair()
    swap(chip(1 - xh, z))
    gb.from_left(True)
    gb.from_right(True)
    gb.from_pair()
    ga.from_far(True)
    swap(chip(xh, far))
    for d in range(1, 8):
        part = q_ref.at[(cc + 8 - d) % 8, k]
        remote(part, part, qs.at[0], qr.at[d], (r, other)).wait_recv()
    half = q_ref.at[:, k]
    copy = remote(half, half, ks.at[0], kr.at[0], (r, other))
    copy.start()
    sent.append(copy)
    ga.from_left(False)
    swap(chip(1 - xh, left))
    ga.from_right(False)
    swap(chip(1 - xh, right))
    gb.from_far(True)
    gb.from_left(False)
    gb.from_right(False)
    ga.from_far(False)
    swap(chip(1 - xh, far))
    gb.from_far(False)
    for chip_index in range(8):
        block = fr_ref.at[chip_index * 2 + 1 - k]
        remote(block, block, cs.at[chip_index], cr.at[chip_index], (r, other)).wait_recv()
    half = q_ref.at[:, 1 - k]
    remote(half, half, ks.at[0], kr.at[0], (r, other)).wait_recv()
    own.wait()
    for copy in sent:
        copy.wait_send()

    @pl.when(r == 7)
    def _():
        for d in range(7):
            remote(last, own_q, qs.at[d], qr.at[0], (d, c)).wait_send()

    @pl.when(jnp.logical_not(diagonal))
    def _():
        for h in range(2):
            remote(
                f_ref.at[:, :, pl.ds(h * COLS, COLS)], fc_ref.at[cc, k], ts.at[h], tr.at[k], (cc, 2 * r + h)
            ).wait_send()

    @pl.when(diagonal)
    def _():
        remote(
            f_ref.at[:, :, pl.ds((1 - k) * COLS, COLS)], fc_ref.at[cc, k], ts.at[0], tr.at[k], (r, other)
        ).wait_send()


def split(x):
    hi = x.astype(BF16)
    return hi, (x - hi.astype(F32)).astype(BF16)


def dot3(a, b, nt=False):
    dims = (((1,), (1 if nt else 0,)), ((), ()))
    (ah, al), (bh, bl) = a, b
    one = lambda u, v: lax.dot_general(u, v, dims, preferred_element_type=F32)
    return one(ah, bh) + (one(ah, bl) + one(al, bh))


def product_kernel(
    rl, pat, w_ref, fr_ref, fc_ref, q_ref, d_ref, x_ref,
    wc, frc, fh, fl, x1, ch, cl, c0h, c0l, ph, pw, acc, rb, cb, rf, cf, wsem, fsem,
):
    r = lax.axis_index("prow")
    c = lax.axis_index("pcol")

    for s in range(2):
        for q in range(CB):
            cf[s, q] = 0

    def scan(p, carry):
        out = []
        for s in range(2):
            n, m = carry[2 * s], carry[2 * s + 1]
            b = rl[0, s, p]
            keep = jnp.where(p < 62, 1, 0)
            lr = b - r * RB
            lc = b - c * CB
            usable = b < NB - 2
            inr = jnp.logical_and(jnp.logical_and(lr >= 0, lr < RB), usable)
            inc = jnp.logical_and(jnp.logical_and(lc >= 0, lc < CB), usable)
            rb[s, n] = lr
            rf[s, n] = keep
            cb[s, m] = lc

            @pl.when(inc)
            def _():
                cf[s, lc] = keep

            out += [n + inr.astype(jnp.int32), m + inc.astype(jnp.int32)]
        return tuple(out)

    zero = jnp.int32(0)
    n0, m0, n1, m1 = lax.fori_loop(0, 64, scan, (zero, zero, zero, zero))
    counts = ((n0, m0), (n1, m1))

    @pl.when(c == 15)
    def _():
        for s in range(2):
            for q in (8, 9):
                cf[s, q] = 1

    def f_copy(s, i):
        return pltpu.make_async_copy(
            fr_ref.at[pl.ds(8 * s, 8), :, :, pl.ds(pl.multiple_of(rb[s, i] * BS, BS), BS)],
            frc.at[s, i], fsem.at[s, i],
        )

    def w_copy(s, i, j):
        return pltpu.make_async_copy(
            w_ref.at[pl.ds(pl.multiple_of(rb[s, i] * BS, BS), BS), pl.ds(pl.multiple_of(cb[s, j] * BS, BS), BS)],
            wc.at[s, pl.ds(pl.multiple_of(i * BS, BS), BS), pl.ds(pl.multiple_of(j * BS, BS), BS)],
            wsem.at[s, i, j],
        )

    for s in range(2):
        n, m = counts[s]

        @pl.loop(0, n)
        def _(i):
            f_copy(s, i).start()

            @pl.loop(0, m)
            def _(j):
                stored = pat[cb[s, j], rb[s, i]] != 0

                @pl.when(stored)
                def _():
                    w_copy(s, i, j).start()

                @pl.when(jnp.logical_not(stored))
                def _():
                    wc[s, pl.ds(pl.multiple_of(i * BS, BS), BS), pl.ds(pl.multiple_of(j * BS, BS), BS)] = jnp.zeros(
                        (BS, BS), F32
                    )

        @pl.when(n % 2 == 1)
        def _():
            frc[s, n] = jnp.zeros((8, 2, 16, BS), F32)
            wc[s, pl.ds(pl.multiple_of(n * BS, BS), BS), :] = jnp.zeros((BS, COLS), F32)

    x_ref[:, pl.ds(0, COLS)] = jnp.zeros((256, COLS), F32)
    x1[...] = jnp.zeros((256, COLS), F32)

    for s in range(2):
        for q in range(CB):
            lanes = pl.ds(q * BS, BS)
            rows = pl.ds(s * BS, BS)
            block = fc_ref[pl.ds(4 * s, 4), :, 1, :, lanes].reshape(BS, BS) * cf[s, q].astype(F32)
            ch[rows, lanes], cl[rows, lanes] = split(block)
            block = fc_ref[pl.ds(4 * s, 4), :, 0, :, lanes].reshape(BS, BS)
            c0h[rows, lanes], c0l[rows, lanes] = split(block)

    for s in range(2):
        n, m = counts[s]

        @pl.loop(0, n)
        def _(i):
            f_copy(s, i).wait()

        @pl.loop(0, (n + 1) // 2)
        def _(i):
            for t in range(2):
                keep = rf[s, 2 * i + t].astype(F32)
                for level in range(2):
                    block = frc[s, 2 * i + t, :, level].reshape(BS, BS)
                    if level == 1:
                        block = block * keep
                    hi, lo = split(block)
                    fh[i, pl.ds(level * BS, BS), pl.ds(t * BS, BS)] = hi
                    fl[i, pl.ds(level * BS, BS), pl.ds(t * BS, BS)] = lo

        @pl.loop(0, n)
        def _(i):
            @pl.loop(0, m)
            def _(j):
                @pl.when(pat[cb[s, j], rb[s, i]] != 0)
                def _():
                    w_copy(s, i, j).wait()

        @pl.loop(0, (m + 1) // 2)
        def _(j):
            acc[...] = jnp.zeros((256, 256), F32)

            @pl.loop(0, (n + 1) // 2)
            def _(i):
                block = wc[
                    s, pl.ds(pl.multiple_of(i * 256, 256), 256), pl.ds(pl.multiple_of(j * 256, 256), 256)
                ]
                acc[...] += dot3((fh[i], fl[i]), split(block))

            for t in range(2):
                @pl.when(2 * j + t < m)
                def _():
                    lanes = pl.ds(pl.multiple_of(cb[s, 2 * j + t] * BS, BS), BS)
                    x_ref[pl.ds(s * BS, BS), lanes] = -acc[pl.ds(0, BS), pl.ds(t * BS, BS)]
                    x1[pl.ds(s * BS, BS), lanes] = acc[pl.ds(BS, BS), pl.ds(t * BS, BS)]

    qv = split(q_ref[...].reshape(256, 256))
    ph[...], pw[...] = split(x_ref[:, pl.ds(0, COLS)])
    pair = lambda h, l, rows: (h[rows, :], l[rows, :])
    whole = pl.ds(0, 256)
    a_t = dot3(pair(ch, cl, whole), pair(ph, pw, whole), nt=True)
    chosen = jnp.where(jnp.logical_and(r == 0, c == 0), 1.0, 0.0).astype(F32)
    s_t = []
    for s in range(2):
        rows = pl.ds(s * BS, BS)
        s_t.append(chosen * d_ref[0, :, rows] - dot3(pair(ph, pw, rows), pair(c0h, c0l, rows), nt=True))
    slot = a_t + jnp.concatenate(
        [dot3((qv[0][:, s * BS:(s + 1) * BS], qv[1][:, s * BS:(s + 1) * BS]), split(s_t[s])) for s in range(2)], axis=1
    )
    a_s, slot_s = split(a_t), split(slot)
    base = 2 * COLS
    for s in range(2):
        rows = pl.ds(s * BS, BS)
        cut = lambda v: (v[0][s * BS:(s + 1) * BS], v[1][s * BS:(s + 1) * BS])
        second = (
            chosen * d_ref[1, :, rows]
            + dot3(split(x1[rows, :]), pair(ch, cl, rows), nt=True)
            + dot3(cut(qv), cut(a_s), nt=True)
            + dot3(cut(slot_s), cut(qv), nt=True)
        )
        x_ref[rows, pl.ds(base, BS)] = s_t[s]
        x_ref[rows, pl.ds(base + BS, BS)] = second
        x_ref[rows, pl.ds(base + 2 * BS, 2 * BS)] = -slot[s * BS:(s + 1) * BS]

    for q in range(0, CB, 2):
        lanes = pl.ds(q * BS, 2 * BS)
        full = x1[:, lanes] + dot3(qv, (ph[:, lanes], pw[:, lanes]))
        for s in range(2):
            for t in range(2):
                part = full[s * BS:(s + 1) * BS, t * BS:(t + 1) * BS]
                x_ref[pl.ds(s * BS, BS), pl.ds(COLS + (q + t) * BS, BS)] = -cf[s, q + t].astype(F32) * part


def reduce_kernel(
    x_ref, panels, diagonals, ax, asum, al, ar, aown, ahl, ahr, yl, yr, yhl, yhr, ysum, yx, fin,
    core, mine, parts, done, xs, xr, rs, rr, ss, sr, cs, cr,
):
    r, c, xl, y, xh, z, k = coords()
    cc = c // 2
    other = c + 1 - 2 * k
    px = (4 * (1 - xl) + y, c)
    right, left, far = (y + 1) % 4, (y + 3) % 4, (y + 2) % 4
    dr, dl = (4 * xl + right, c), (4 * xl + left, c)
    barrier = pltpu.get_barrier_semaphore()
    for device in [px, dr, dl, (r, other)] + [(r, ((cc + d) % 8) * 2 + k) for d in range(1, 8)]:
        pl.semaphore_signal(barrier, inc=1, device_id=device, device_id_type=MESH)
    pl.semaphore_wait(barrier, 11)
    sent = []

    def push(src, dst, send, recv, device):
        copy = remote(src, dst, send, recv, device)
        copy.start()
        sent.append(copy)

    def arrived(ref, send, recv):
        remote(ref, ref, send, recv, px).wait_recv()

    def rows(p, w, h=None):
        if h is None:
            return pl.ds(pl.multiple_of((4 * p + w) * 32, 32), 32)
        return pl.ds(pl.multiple_of((4 * p + w) * 32 + 16 * h, 16), 16)

    lane_a = pl.ds(0, COLS)
    streams = ((2 * COLS, SMALL), (COLS, COLS))

    def ring_first(t, p, v):
        start, width = streams[t]
        lanes = pl.ds(start, width)
        e = 2 * t + v
        push(x_ref.at[rows(p, far, 0), lanes], yhl[t].at[v], rs.at[e, 0], rr.at[e, 0], dr)
        push(x_ref.at[rows(p, far, 1), lanes], yhr[t].at[v], rs.at[e, 1], rr.at[e, 1], dl)

    def ring_second(t, p, v):
        start, width = streams[t]
        lanes = pl.ds(start, width)
        e = 2 * t + v
        arrived(yhl[t].at[v], rs.at[e, 0], rr.at[e, 0])
        low = x_ref[rows(p, right, 0), lanes] + yhl[t][v]
        ysum[t][v, 0, pl.ds(0, 16), :] = low
        ysum[t][v, 0, pl.ds(16, 16), :] = x_ref[rows(p, right, 1), lanes]
        push(ysum[t].at[v, 0], yl[t].at[v], rs.at[e, 2], rr.at[e, 2], dr)
        arrived(yhr[t].at[v], rs.at[e, 1], rr.at[e, 1])
        ysum[t][v, 1, pl.ds(0, 16), :] = x_ref[rows(p, left, 0), lanes]
        ysum[t][v, 1, pl.ds(16, 16), :] = x_ref[rows(p, left, 1), lanes] + yhr[t][v]
        push(ysum[t].at[v, 1], yr[t].at[v], rs.at[e, 3], rr.at[e, 3], dl)

    def ring_third(t, p, v):
        start, width = streams[t]
        e = 2 * t + v
        arrived(yl[t].at[v], rs.at[e, 2], rr.at[e, 2])
        arrived(yr[t].at[v], rs.at[e, 3], rr.at[e, 3])
        return x_ref[rows(p, y), pl.ds(start, width)] + (yl[t][v] + yr[t][v])

    q = 1 - xl
    ring_first(0, q, 0)
    ring_first(0, xl, 1)
    for w, d in ((0, far), (1, right), (2, left), (3, y)):
        push(x_ref.at[rows(q, d), lane_a], ax.at[w], xs.at[w], xr.at[w], px)
    ring_first(1, q, 0)
    ring_second(0, q, 0)
    ring_second(0, xl, 1)
    ring_first(1, xl, 1)
    ring_second(1, q, 0)

    fin[0][...] = ring_third(0, q, 0)
    push(fin[0], yx[0], xs.at[4], xr.at[4], px)
    ring_second(1, xl, 1)

    arrived(ax.at[0], xs.at[0], xr.at[0])
    asum[0] = x_ref[rows(xl, far), lane_a] + ax[0]
    push(asum.at[0, pl.ds(0, 16)], ahl, rs.at[4, 0], rr.at[4, 0], dr)
    push(asum.at[0, pl.ds(16, 16)], ahr, rs.at[4, 1], rr.at[4, 1], dl)

    small = ring_third(0, xl, 1)
    arrived(yx[0], xs.at[4], xr.at[4])
    mine[...] = small + yx[0][...]
    push(mine, core, cs.at[0], cr.at[0], (r, other))

    arrived(ax.at[1], xs.at[1], xr.at[1])
    asum[1] = x_ref[rows(xl, right), lane_a] + ax[1]
    arrived(ahl, rs.at[4, 0], rr.at[4, 0])
    asum[1, pl.ds(0, 16)] = asum[1, pl.ds(0, 16)] + ahl[...]
    push(asum.at[1], al, rs.at[4, 2], rr.at[4, 2], dr)

    arrived(core, cs.at[0], cr.at[0])
    own_half = pl.ds(pl.multiple_of(16 * k, 16), 16)
    parts[cc] = mine[own_half, :] + core[own_half, :]
    for d in range(1, 8):
        push(parts.at[cc], parts.at[cc], ss.at[d], sr.at[d], (r, ((cc + d) % 8) * 2 + k))

    arrived(ax.at[2], xs.at[2], xr.at[2])
    asum[2] = x_ref[rows(xl, left), lane_a] + ax[2]
    arrived(ahr, rs.at[4, 1], rr.at[4, 1])
    asum[2, pl.ds(16, 16)] = asum[2, pl.ds(16, 16)] + ahr[...]
    push(asum.at[2], ar, rs.at[4, 3], rr.at[4, 3], dl)

    fin[1][...] = ring_third(1, q, 0)
    push(fin[1], yx[1], xs.at[5], xr.at[5], px)

    for d in range(1, 8):
        arrived(parts.at[(cc + 8 - d) % 8], ss.at[d], sr.at[d])
    total = parts[0]
    for d in range(1, 8):
        total = total + parts[d]
    done[own_half, :] = total
    push(done.at[own_half], done.at[own_half], cs.at[1], cr.at[1], (r, other))

    arrived(ax.at[3], xs.at[3], xr.at[3])
    first = x_ref[rows(xl, y), lane_a] + ax[3]
    second = ring_third(1, xl, 1)
    arrived(al, rs.at[4, 2], rr.at[4, 2])
    arrived(ar, rs.at[4, 3], rr.at[4, 3])
    panels[0] = first + (al[...] + ar[...])
    arrived(yx[1], xs.at[5], xr.at[5])
    panels[1] = second + yx[1][...]
    other_half = pl.ds(pl.multiple_of(16 * (1 - k), 16), 16)
    arrived(done.at[other_half], cs.at[1], cr.at[1])
    diagonals[0] = done[:, pl.ds(0, BS)]
    diagonals[1] = done[:, pl.ds(BS, BS)]
    at_end = jnp.where(c == 15, 1.0, 0.0).astype(F32)
    tail = pl.ds(COLS - 2 * BS, 2 * BS)
    panels[1, :, tail] = panels[1, :, tail] + at_end * done[:, pl.ds(2 * BS, 2 * BS)]
    for copy in sent:
        copy.wait_send()


def local(window, pattern, row_lists, factor, diag_inverse):
    dma = pltpu.SemaphoreType.DMA
    hbm = pl.BlockSpec(memory_space=pl.ANY)
    vmem = pl.BlockSpec(memory_space=pltpu.VMEM)
    smem = pl.BlockSpec(memory_space=pltpu.SMEM)
    f_t = jnp.swapaxes(factor, 1, 2)
    fr, fc, q_t = pl.pallas_call(
        gather_kernel,
        out_shape=(
            jax.ShapeDtypeStruct((16, 2, 16, ROWS), F32),
            jax.ShapeDtypeStruct((8, 2, 2, 16, COLS), F32),
            jax.ShapeDtypeStruct((8, 2, 16, 2 * BS), F32),
        ),
        in_specs=[hbm],
        out_specs=(hbm, hbm, hbm),
        scratch_shapes=[
            dma((9,)), dma((9,)), dma((9,)), dma((9,)), dma((8,)), dma((8,)), dma((2,)), dma((2,)),
            dma((15,)), dma((8,)), dma((1,)), dma((1,)), dma((3,)),
        ],
        compiler_params=pltpu.CompilerParams(collective_id=0, has_side_effects=True),
        name="gather_factor",
    )(f_t)
    x = pl.pallas_call(
        product_kernel,
        out_shape=jax.ShapeDtypeStruct((256, LANES), F32),
        in_specs=[smem, smem, hbm, hbm, vmem, vmem, vmem],
        out_specs=vmem,
        scratch_shapes=[
            pltpu.VMEM((2, ROWS, COLS), F32),
            pltpu.VMEM((2, RB, 8, 2, 16, BS), F32),
            pltpu.VMEM((RB // 2, 256, 256), BF16),
            pltpu.VMEM((RB // 2, 256, 256), BF16),
            pltpu.VMEM((256, COLS), F32),
            pltpu.VMEM((256, COLS), BF16),
            pltpu.VMEM((256, COLS), BF16),
            pltpu.VMEM((256, COLS), BF16),
            pltpu.VMEM((256, COLS), BF16),
            pltpu.VMEM((256, COLS), BF16),
            pltpu.VMEM((256, COLS), BF16),
            pltpu.VMEM((256, 256), F32),
            pltpu.SMEM((2, RB + 4), jnp.int32),
            pltpu.SMEM((2, CB + 6), jnp.int32),
            pltpu.SMEM((2, RB + 4), jnp.int32),
            pltpu.SMEM((2, CB + 6), jnp.int32),
            dma((2, RB, CB)),
            dma((2, RB)),
        ],
        compiler_params=pltpu.CompilerParams(vmem_limit_bytes=60 * 1024 * 1024),
        name="products",
    )(row_lists, jnp.swapaxes(pattern, 0, 1), window, fr, fc, q_t, diag_inverse)
    v = lambda *shape: pltpu.VMEM(shape, F32)
    panels, diagonals = pl.pallas_call(
        reduce_kernel,
        out_shape=(
            jax.ShapeDtypeStruct((2, 32, COLS), F32),
            jax.ShapeDtypeStruct((2, 32, BS), F32),
        ),
        in_specs=[vmem],
        out_specs=(vmem, vmem),
        scratch_shapes=[
            v(4, 32, COLS), v(3, 32, COLS), v(32, COLS), v(32, COLS), v(32, COLS), v(16, COLS), v(16, COLS),
            [v(2, 32, SMALL), v(2, 32, COLS)], [v(2, 32, SMALL), v(2, 32, COLS)],
            [v(2, 16, SMALL), v(2, 16, COLS)], [v(2, 16, SMALL), v(2, 16, COLS)],
            [v(2, 2, 32, SMALL), v(2, 2, 32, COLS)],
            [v(32, SMALL), v(32, COLS)], [v(32, SMALL), v(32, COLS)],
            v(32, SMALL), v(32, SMALL), v(8, 16, SMALL), v(32, SMALL),
            dma((6,)), dma((6,)), dma((5, 4)), dma((5, 4)), dma((8,)), dma((8,)), dma((2,)), dma((2,)),
        ],
        compiler_params=pltpu.CompilerParams(collective_id=1, has_side_effects=True),
        name="reduce_sums",
    )(x)
    return jnp.swapaxes(panels, 1, 2), jnp.swapaxes(diagonals, 1, 2)


def solution(mesh):
    in_specs = (P("prow", "pcol"), P("prow", "pcol"), P(), P(None, "prow", "pcol"), P())
    out_specs = (P(None, "pcol", "prow"), P(None, None, "prow"))
    return jax.shard_map(local, mesh=mesh, in_specs=in_specs, out_specs=out_specs, check_vma=False)
```

time: 470 us -> 119 us (0.25)
  waiting for transfers between devices: 226 us -> 0 us
  blocking collectives: 131 us -> 0 us
  Pallas kernels: 0 us -> 114 us
  matrix products: 55.4 us -> 0 us
  local copies, waits for them, and re-layouts: 26.8 us -> 3.09 us
  between operations: 14.3 us -> 0.65 us
  other arithmetic: 11.4 us -> 0 us
    psum x2 -> x0, blocking collectives: 131 us -> none  [local(): gram_piece = lax.psum(product_first(owned_cols, solved), 'pcol')]
    pallas_call x0 -> x3, Pallas kernels: none -> 114 us  [the longest x1 51.1 us: local(): pl.pallas_call(gather_kernel, out_shape=(jax.ShapeDtypeStruct((16, 2, 16,...]
    all_gather x3 -> x0, waiting for transfers between devices: 86.9 us -> none  [the longest x2 49.6 us: local(): live_rows = lax.all_gather(live_factor, 'pcol', axis=1, tiled=True)]
    reduce_scatter x2 -> x0, waiting for transfers between devices: 70 us -> none  [local(): lax.psum_scatter(partial_value, 'prow', scatter_dimension=1, tiled=True)]
    psum x1 -> x0, waiting for transfers between devices: 68.2 us -> none  [local(): live_cols = lax.psum(mirror_rows(live_rows, local_cols), 'prow')]
    dot_general x7 -> x0, matrix products: 55.4 us -> none  [the longest x5 49.3 us: product_first(): lax.dot_general(left_side, right_side, (((0,), (0,)), ((), ())), precisio...]
    unnamed x15 -> x2, local copies, waits for them, and re-layouts: 15.3 us -> 3.09 us
    mul x5 -> x0, local copies, waits for them, and re-layouts: 9.35 us -> none  [the longest x1 9.04 us: local(): window.reshape(row_blocks, BS, col_blocks, BS) * keeper[:, None, :, None]]
  transfers between devices with their start and end apart: 6 -> 0, of which waited for: 6 -> 0; matrix products, arithmetic and copies ran while one was open for 17% -> 0% of each run, Pallas kernels for 0% -> 0%
where the time goes in v1:
time: 119 us; the launch traced here: 118 us
  Pallas kernels  114 us (96%)
  local copies, waits for them, and re-layouts  3.09 us (3%)
    pallas_call x1, Pallas kernels, local(): pl.pallas_call(gather_kernel, out_shape=(jax.ShapeDtypeStruct((16, 2, 16,...  51.1 us
    pallas_call x1, Pallas kernels, local(): pl.pallas_call(reduce_kernel, out_shape=(jax.ShapeDtypeStruct((2, 32, COL...  44.5 us
    pallas_call x1, Pallas kernels, local(): pl.pallas_call(product_kernel, out_shape=jax.ShapeDtypeStruct((256, LANES...  18.3 us
    unnamed x2, local copies, waits for them, and re-layouts  3.09 us

profile of v1, /device:TPU:1, one launch (start us, length us, event | category | flops | bytes accessed | tf_op | source)
XLA Modules:
  0.0 117.6 jit_solution(4348670547852179096)
XLA Ops:
  0.6 51.1 %gather_factor.1 = (f32[16,2,16,2560]{3,2,1,0:T(8,128)}, f32[8,2,2,16,1280]{4,3,2,1,0:T(8,128)}, f32[8,2,16,256]{3,2,1,0:T(8,128)}) custom-call(f32[2,16,2560]{2,1,0:T(8,128)} %bitcast.4), custom_call_target="tpu_custom_call" | custom-call | tf_op jit(solution)/shard_map/gather_factor/pallas_call | solution.py:567
  51.8 18.3 %products.1.x_ref = f32[256,3072]{1,0:T(8,128)} custom-call(s32[2,2,64]{2,1,0:T(2,128)} %rl.1, s32[10,20]{1,0:T(8,128)} %bitcast.7, f32[2560,1280]{1,0:T(8,128)} %w_ref.1, f32[16,2,16,2560]{3,2,1,0:T(8,128)} %get-tuple-element.7.fr_ref, f32[8,2,2,16,1280]{4,3,2,1,0:T(8,128)} %get-tuple-element.8.fc_ref, f32[8,2,16,256]{3,2,1,0:T(8,128)} %get-tuple-element.9.q_ref, ...), custom_call_target="tpu_custom_call" | custom-call | tf_op jit(solution)/shard_map/products/pallas_call | solution.py:583
  70.0 44.5 %reduce_sums.1 = (f32[2,32,1280]{2,1,0:T(8,128)}, f32[2,32,128]{2,1,0:T(8,128)}) custom-call(f32[256,3072]{1,0:T(8,128)} %products.1.x_ref), custom_call_target="tpu_custom_call" | custom-call | tf_op jit(solution)/shard_map/reduce_sums/pallas_call | solution.py:612
  114.5 1.7 %copy.9 = f32[2,1280,32]{1,2,0:T(8,128)} copy(f32[2,1280,32]{1,2,0:T(8,128)} %bitcast.5) | data formatting | bytes 655360
  116.2 1.4 %copy.10 = f32[2,128,32]{1,2,0:T(8,128)} copy(f32[2,128,32]{1,2,0:T(8,128)} %bitcast.6) | data formatting | bytes 65536

commit v2 on v0

v2 whole, which is shorter than its diff:
```python
import jax
import jax.numpy as jnp
from jax import lax
from jax.experimental import pallas as pl
from jax.experimental.pallas import tpu as pltpu
from jax.sharding import PartitionSpec as P

BS = 128
NB = 160
RB = 20
CB = 10
ROWS = RB * BS
COLS = CB * BS
SMALL = 512
LANES = 2 * COLS + SMALL
MESH = pl.DeviceIdType.MESH
F32 = jnp.float32
BF16 = jnp.bfloat16


def remote(src, dst, send, recv, device):
    return pltpu.make_async_remote_copy(
        src_ref=src, dst_ref=dst, send_sem=send, recv_sem=recv, device_id=device, device_id_type=MESH
    )


def coords():
    r = lax.axis_index("prow")
    c = lax.axis_index("pcol")
    return r, c, r // 4, r % 4, c // 8, (c // 2) % 4, c % 2


class PairRing:
    def __init__(self, send, recv, block, half, device, p, y, sent):
        self.s, self.r, self.block, self.half, self.device = send, recv, block, half, device
        self.p, self.y, self.sent = p, y, sent
        self.q = 1 - p
        self.right, self.left, self.far = (y + 1) % 4, (y + 3) % 4, (y + 2) % 4

    def push(self, k, src, dst, device):
        copy = remote(src, dst, self.s.at[k], self.r.at[k], device)
        copy.start()
        self.sent.append(copy)

    def wait(self, k, ref):
        remote(ref, ref, self.s.at[k], self.r.at[k], self.device(self.p, self.right)).wait_recv()

    def start(self, src):
        own = self.block(self.p, self.y)
        self.push(0, src, own, self.device(self.q, self.y))
        self.push(1, src, own, self.device(self.p, self.right))
        self.push(2, src, own, self.device(self.p, self.left))

    def from_left(self, own):
        k, p = (1, self.p) if own else (5, self.q)
        self.wait(k, self.block(p, self.left))
        part = self.half(p, self.left, 0)
        self.push(k + 2, part, part, self.device(self.p, self.right))

    def from_right(self, own):
        k, p = (2, self.p) if own else (6, self.q)
        self.wait(k, self.block(p, self.right))
        part = self.half(p, self.right, 1)
        self.push(k + 2, part, part, self.device(self.p, self.left))

    def from_pair(self):
        other = self.block(self.q, self.y)
        self.wait(0, other)
        self.push(5, other, other, self.device(self.p, self.right))
        self.push(6, other, other, self.device(self.p, self.left))

    def from_far(self, own):
        k, p = (3, self.p) if own else (7, self.q)
        self.wait(k, self.half(p, self.far, 0))
        self.wait(k + 1, self.half(p, self.far, 1))


def split(x):
    hi = x.astype(BF16)
    return hi, (x - hi.astype(F32)).astype(BF16)


def dot3(a, b, nt=False):
    dims = (((1,), (1 if nt else 0,)), ((), ()))
    (ah, al), (bh, bl) = a, b
    one = lambda u, v: lax.dot_general(u, v, dims, preferred_element_type=F32)
    return one(ah, bh) + (one(ah, bl) + one(al, bh))


def kernel(
    rl_ref, pat, w_ref, f_ref, d_ref, panels, diagonals,
    fr, fc, q_ref, w_all, wh, wl, fh, fl, mr, mc, x_ref, x1, ch, cl, c0h, c0l, ph, pw, acc,
    ax, asum, al, ar, ahl, ahr, yl, yr, yhl, yhr, ysum, yx, fin, core, mine, parts, done,
    as_, ar_, bs, br, cs, cr, ts, tr, qs, qr, ks, kr, wsem, local_sem,
    xs, xr, rs, rr, ss, sr, hs, hr,
):
    r, c, xl, y, xh, z, k = coords()
    cc = c // 2
    other = c + 1 - 2 * k
    partner = (r, other)
    diagonal = r == cc
    off_diagonal = jnp.logical_not(diagonal)
    barrier = pltpu.get_barrier_semaphore()

    def greet(device):
        pl.semaphore_signal(barrier, inc=1, device_id=device, device_id_type=MESH)

    @pl.when(off_diagonal)
    def _():
        greet((cc, 2 * r))
        greet((cc, 2 * r + 1))

    for d in range(1, 8):
        greet((r, ((cc + d) % 8) * 2 + k))
        greet(((r + d) % 8, c))
    greet(partner)

    def w_copy(i):
        rows = pl.ds(i * 2 * BS, 2 * BS)
        return pltpu.make_async_copy(w_ref.at[rows], w_all.at[rows], wsem.at[i])

    for i in range(RB // 2):
        w_copy(i).start()

    def mark(dst, first):
        def body(b, carry):
            lanes = pl.ds(pl.multiple_of(b * BS, BS), BS)
            for level in range(2):
                hit = jnp.where(rl_ref[level] == first + b, 1.0, 0.0).astype(F32)
                dst[level, :, lanes] = jnp.broadcast_to(jnp.max(hit, axis=1, keepdims=True), (2, BS))
            return carry

        return body

    lax.fori_loop(0, RB, mark(mr, r * RB), 0)
    lax.fori_loop(0, CB, mark(mc, c * CB), 0)

    @pl.when(off_diagonal)
    def _():
        pl.semaphore_wait(barrier, 17)

    @pl.when(diagonal)
    def _():
        pl.semaphore_wait(barrier, 15)

    sent = []

    def push(src, dst, send, recv, device):
        copy = remote(src, dst, send, recv, device)
        copy.start()
        sent.append(copy)

    def arrived(ref, send, recv):
        remote(ref, ref, send, recv, partner).wait_recv()

    def row_gather(level):
        return PairRing(
            as_.at[level], ar_.at[level],
            lambda p, w: fr.at[level, p * 8 + w * 2 + k],
            lambda p, w, h: fr.at[level, p * 8 + w * 2 + k, pl.ds(8 * h, 8)],
            lambda p, w: (r, p * 8 + w * 2 + k),
            xh, z, sent,
        )

    def column_gather(level):
        return PairRing(
            bs.at[level], br.at[level],
            lambda p, w: fc.at[level, p * 4 + w],
            lambda p, w, h: fc.at[level, p * 4 + w, h],
            lambda p, w: (p * 4 + w, c),
            xl, y, sent,
        )

    ga = [row_gather(0), row_gather(1)]
    gb = [column_gather(0), column_gather(1)]

    def across(level, h):
        return remote(
            f_ref.at[level, :, pl.ds(h * COLS, COLS)], fc.at[level, cc, k], ts.at[level, h], tr.at[level, k],
            (cc, 2 * r + h),
        )

    def across_chip(level):
        return remote(
            f_ref.at[level, :, pl.ds((1 - k) * COLS, COLS)], fc.at[level, cc, k], ts.at[level, 0], tr.at[level, k],
            partner,
        )

    def across_own(level):
        return pltpu.make_async_copy(
            f_ref.at[level, :, pl.ds(k * COLS, COLS)], fc.at[level, r, k], local_sem.at[2 + level]
        )

    @pl.when(off_diagonal)
    def _():
        for level in range(2):
            for h in range(2):
                across(level, h).start()

    @pl.when(diagonal)
    def _():
        for level in range(2):
            across_chip(level).start()
            across_own(level).start()

    last = f_ref.at[1, :, pl.ds(ROWS - 2 * BS, 2 * BS)]
    own_q = q_ref.at[cc, k]

    @pl.when(r == 7)
    def _():
        pltpu.make_async_copy(last, own_q, local_sem.at[0]).start()
        for d in range(7):
            remote(last, own_q, qs.at[d], qr.at[0], (d, c)).start()

    own_copy = [pltpu.make_async_copy(f_ref.at[level], fr.at[level, c], local_sem.at[4 + level]) for level in range(2)]
    for copy in own_copy:
        copy.start()

    def swap(level, chip, src=None):
        block = fr.at[level, chip * 2 + k]
        push(block if src is None else src, block, cs.at[level, chip], cr.at[level, chip], partner)

    right, left, far = (z + 1) % 4, (z + 3) % 4, (z + 2) % 4
    chip = lambda p, w: p * 4 + w

    def row_step(level, step, own):
        side = xh if own else 1 - xh
        if step == "left":
            ga[level].from_left(own)
            swap(level, chip(side, left))
        elif step == "right":
            ga[level].from_right(own)
            swap(level, chip(side, right))
        elif step == "far":
            ga[level].from_far(own)
            swap(level, chip(side, far))
        else:
            ga[level].from_pair()
            swap(level, chip(1 - xh, z))

    def column_start(level):
        @pl.when(off_diagonal)
        def _():
            for h in range(2):
                arrived(fc.at[level, r, h], ts.at[level, h], tr.at[level, h])

        @pl.when(diagonal)
        def _():
            arrived(fc.at[level, r, 1 - k], ts.at[level, 0], tr.at[level, 1 - k])
            across_own(level).wait()

        gb[level].start(fc.at[level, r])

    def split_window(i0, i1):
        for i in range(i0, i1):
            w_copy(i).wait()

        def body(i, carry):
            rows = pl.ds(pl.multiple_of(i * BS, BS), BS)
            row_ok = jnp.where(r * RB + i < NB - 2, 1, 0)
            for j in range(CB):
                lanes = pl.ds(j * BS, BS)
                ok = jnp.where(c * CB + j < NB - 2, 1, 0)
                keep = (pat[j, i] * row_ok * ok).astype(F32)
                wh[rows, lanes], wl[rows, lanes] = split(w_all[rows, lanes] * keep)
            return carry

        lax.fori_loop(2 * i0, 2 * i1, body, 0)

    def split_rows(level):
        def body(b, carry):
            lanes = pl.ds(pl.multiple_of(b * BS, BS), BS)
            for s in range(2):
                rows = pl.ds(s * BS, BS)
                block = fr[level, pl.ds(8 * s, 8), :, lanes].reshape(BS, BS) * mr[level, pl.ds(s, 1), lanes]
                fh[rows, lanes], fl[rows, lanes] = split(block)
            return carry

        lax.fori_loop(0, RB, body, 0)

    def product(n):
        acc[...] = jnp.zeros((256, 256), F32)
        lanes = pl.ds(n * 256, 256)

        def body(i, carry):
            depth = pl.ds(pl.multiple_of(i * 512, 512), 512)
            acc[...] += dot3((fh[:, depth], fl[:, depth]), (wh[depth, lanes], wl[depth, lanes]))
            return carry

        lax.fori_loop(0, RB // 4, body, 0)

    def first_level(n):
        product(n)
        lanes = pl.ds(n * 256, 256)
        for s in range(2):
            rows = pl.ds(s * BS, BS)
            x_ref[rows, lanes] = -(acc[rows, :] * mc[0, pl.ds(s, 1), lanes])

    def second_level(n):
        product(n)
        x1[:, pl.ds(n * 256, 256)] = acc[...]

    ga[0].start(f_ref.at[0])
    swap(0, cc, f_ref.at[0])
    split_window(0, 4)

    @pl.when(r == 7)
    def _():
        pltpu.make_async_copy(last, own_q, local_sem.at[0]).wait()

    @pl.when(r != 7)
    def _():
        arrived(own_q, qs.at[0], qr.at[0])

    for d in range(1, 8):
        push(own_q, own_q, qs.at[7 + d], qr.at[d], (r, ((cc + d) % 8) * 2 + k))
    row_step(0, "left", True)
    row_step(0, "right", True)
    ga[1].start(f_ref.at[1])
    swap(1, cc, f_ref.at[1])
    column_start(0)
    column_start(1)
    row_step(0, "pair", True)
    split_window(4, 7)
    gb[0].from_left(True)
    gb[0].from_right(True)
    row_step(0, "far", True)
    row_step(1, "left", True)
    row_step(1, "right", True)
    gb[0].from_pair()
    row_step(1, "pair", True)
    gb[1].from_left(True)
    gb[1].from_right(True)
    row_step(0, "left", False)
    row_step(0, "right", False)
    split_window(7, 10)
    gb[1].from_pair()
    gb[0].from_far(True)
    gb[0].from_left(False)
    gb[0].from_right(False)
    row_step(1, "far", True)
    row_step(0, "far", False)
    for d in range(1, 8):
        arrived(q_ref.at[(cc + 8 - d) % 8, k], qs.at[0], qr.at[d])
    half = q_ref.at[:, k]
    push(half, half, ks.at[0], kr.at[0], partner)
    for m in range(8):
        arrived(fr.at[0, m * 2 + 1 - k], cs.at[0, m], cr.at[0, m])
    own_copy[0].wait()

    split_rows(0)
    first_level(0)
    row_step(1, "left", False)
    row_step(1, "right", False)
    first_level(1)
    gb[1].from_far(True)
    gb[1].from_left(False)
    gb[1].from_right(False)
    first_level(2)
    gb[0].from_far(False)
    row_step(1, "far", False)
    first_level(3)
    first_level(4)

    px = (4 * (1 - xl) + y, c)
    yright, yleft, yfar = (y + 1) % 4, (y + 3) % 4, (y + 2) % 4
    dr, dl = (4 * xl + yright, c), (4 * xl + yleft, c)

    def rows_of(p, w, h=None):
        if h is None:
            return pl.ds(pl.multiple_of((4 * p + w) * 32, 32), 32)
        return pl.ds(pl.multiple_of((4 * p + w) * 32 + 16 * h, 16), 16)

    lane_a = pl.ds(0, COLS)
    streams = ((2 * COLS, SMALL), (COLS, COLS))

    def ring_first(t, p, v):
        start, width = streams[t]
        lanes = pl.ds(start, width)
        e = 2 * t + v
        push(x_ref.at[rows_of(p, yfar, 0), lanes], yhl[t].at[v], rs.at[e, 0], rr.at[e, 0], dr)
        push(x_ref.at[rows_of(p, yfar, 1), lanes], yhr[t].at[v], rs.at[e, 1], rr.at[e, 1], dl)

    def ring_second(t, p, v):
        start, width = streams[t]
        lanes = pl.ds(start, width)
        e = 2 * t + v
        arrived(yhl[t].at[v], rs.at[e, 0], rr.at[e, 0])
        ysum[t][v, 0, pl.ds(0, 16), :] = x_ref[rows_of(p, yright, 0), lanes] + yhl[t][v]
        ysum[t][v, 0, pl.ds(16, 16), :] = x_ref[rows_of(p, yright, 1), lanes]
        push(ysum[t].at[v, 0], yl[t].at[v], rs.at[e, 2], rr.at[e, 2], dr)
        arrived(yhr[t].at[v], rs.at[e, 1], rr.at[e, 1])
        ysum[t][v, 1, pl.ds(0, 16), :] = x_ref[rows_of(p, yleft, 0), lanes]
        ysum[t][v, 1, pl.ds(16, 16), :] = x_ref[rows_of(p, yleft, 1), lanes] + yhr[t][v]
        push(ysum[t].at[v, 1], yr[t].at[v], rs.at[e, 3], rr.at[e, 3], dl)

    def ring_third(t, p, v):
        start, width = streams[t]
        e = 2 * t + v
        arrived(yl[t].at[v], rs.at[e, 2], rr.at[e, 2])
        arrived(yr[t].at[v], rs.at[e, 3], rr.at[e, 3])
        return x_ref[rows_of(p, y), pl.ds(start, width)] + (yl[t][v] + yr[t][v])

    q = 1 - xl
    for w, d in ((0, yfar), (1, yright), (2, yleft), (3, y)):
        push(x_ref.at[rows_of(q, d), lane_a], ax.at[w], xs.at[w], xr.at[w], px)

    for m in range(8):
        arrived(fr.at[1, m * 2 + 1 - k], cs.at[1, m], cr.at[1, m])
    own_copy[1].wait()
    split_rows(1)
    second_level(0)
    arrived(ax.at[0], xs.at[0], xr.at[0])
    asum[0] = x_ref[rows_of(xl, yfar), lane_a] + ax[0]
    push(asum.at[0, pl.ds(0, 16)], ahl, rs.at[4, 0], rr.at[4, 0], dr)
    push(asum.at[0, pl.ds(16, 16)], ahr, rs.at[4, 1], rr.at[4, 1], dl)
    second_level(1)
    gb[1].from_far(False)
    second_level(2)
    arrived(ax.at[1], xs.at[1], xr.at[1])
    asum[1] = x_ref[rows_of(xl, yright), lane_a] + ax[1]
    arrived(ahl, rs.at[4, 0], rr.at[4, 0])
    asum[1, pl.ds(0, 16)] = asum[1, pl.ds(0, 16)] + ahl[...]
    push(asum.at[1], al, rs.at[4, 2], rr.at[4, 2], dr)
    second_level(3)
    arrived(ax.at[2], xs.at[2], xr.at[2])
    asum[2] = x_ref[rows_of(xl, yleft), lane_a] + ax[2]
    arrived(ahr, rs.at[4, 1], rr.at[4, 1])
    asum[2, pl.ds(16, 16)] = asum[2, pl.ds(16, 16)] + ahr[...]
    push(asum.at[2], ar, rs.at[4, 3], rr.at[4, 3], dl)
    second_level(4)

    for s in range(2):
        rows = pl.ds(s * BS, BS)

        def body(j, carry):
            lanes = pl.ds(pl.multiple_of(j * BS, BS), BS)
            block = fc[1, pl.ds(4 * s, 4), :, :, lanes].reshape(BS, BS) * mc[1, pl.ds(s, 1), lanes]
            ch[rows, lanes], cl[rows, lanes] = split(block)
            block = fc[0, pl.ds(4 * s, 4), :, :, lanes].reshape(BS, BS)
            c0h[rows, lanes], c0l[rows, lanes] = split(block)
            return carry

        lax.fori_loop(0, CB, body, 0)
    half = q_ref.at[:, 1 - k]
    arrived(half, ks.at[0], kr.at[0])
    qv = split(q_ref[...].reshape(256, 256))
    ph[...], pw[...] = split(x_ref[:, lane_a])
    pair = lambda h, l, rows: (h[rows, :], l[rows, :])
    whole = pl.ds(0, 256)
    a_t = dot3(pair(ch, cl, whole), pair(ph, pw, whole), nt=True)
    chosen = jnp.where(jnp.logical_and(r == 0, c == 0), 1.0, 0.0).astype(F32)
    s_t = []
    for s in range(2):
        rows = pl.ds(s * BS, BS)
        s_t.append(chosen * d_ref[0, :, rows] - dot3(pair(ph, pw, rows), pair(c0h, c0l, rows), nt=True))
    slot = a_t + jnp.concatenate(
        [dot3((qv[0][:, s * BS:(s + 1) * BS], qv[1][:, s * BS:(s + 1) * BS]), split(s_t[s])) for s in range(2)], axis=1
    )
    a_s, slot_s = split(a_t), split(slot)
    base = 2 * COLS
    for s in range(2):
        rows = pl.ds(s * BS, BS)
        cut = lambda v: (v[0][s * BS:(s + 1) * BS], v[1][s * BS:(s + 1) * BS])
        second = (
            chosen * d_ref[1, :, rows]
            + dot3(split(x1[rows, :]), pair(ch, cl, rows), nt=True)
            + dot3(cut(qv), cut(a_s), nt=True)
            + dot3(cut(slot_s), cut(qv), nt=True)
        )
        x_ref[rows, pl.ds(base, BS)] = s_t[s]
        x_ref[rows, pl.ds(base + BS, BS)] = second
        x_ref[rows, pl.ds(base + 2 * BS, 2 * BS)] = -slot[s * BS:(s + 1) * BS]
    ring_first(0, q, 0)
    ring_first(0, xl, 1)

    def second_sum(n, carry):
        lanes = pl.ds(pl.multiple_of(n * 256, 256), 256)
        full = x1[:, lanes] + dot3(qv, (ph[:, lanes], pw[:, lanes]))
        out = pl.ds(pl.multiple_of(COLS + n * 256, 256), 256)
        for s in range(2):
            x_ref[pl.ds(s * BS, BS), out] = -(full[s * BS:(s + 1) * BS] * mc[1, pl.ds(s, 1), lanes])
        return carry

    lax.fori_loop(0, CB // 2, second_sum, 0)
    ring_first(1, q, 0)
    ring_second(0, q, 0)
    ring_second(0, xl, 1)
    ring_first(1, xl, 1)
    ring_second(1, q, 0)

    fin[0][...] = ring_third(0, q, 0)
    push(fin[0], yx[0], xs.at[4], xr.at[4], px)
    ring_second(1, xl, 1)
    small = ring_third(0, xl, 1)
    arrived(yx[0], xs.at[4], xr.at[4])
    mine[...] = small + yx[0][...]
    push(mine, core, hs.at[0], hr.at[0], partner)
    arrived(core, hs.at[0], hr.at[0])
    own_half = pl.ds(pl.multiple_of(16 * k, 16), 16)
    parts[cc] = mine[own_half, :] + core[own_half, :]
    for d in range(1, 8):
        push(parts.at[cc], parts.at[cc], ss.at[d], sr.at[d], (r, ((cc + d) % 8) * 2 + k))

    fin[1][...] = ring_third(1, q, 0)
    push(fin[1], yx[1], xs.at[5], xr.at[5], px)

    arrived(ax.at[3], xs.at[3], xr.at[3])
    first = x_ref[rows_of(xl, y), lane_a] + ax[3]
    arrived(al, rs.at[4, 2], rr.at[4, 2])
    arrived(ar, rs.at[4, 3], rr.at[4, 3])
    panels[0] = first + (al[...] + ar[...])

    for d in range(1, 8):
        arrived(parts.at[(cc + 8 - d) % 8], ss.at[d], sr.at[d])
    total = parts[0]
    for d in range(1, 8):
        total = total + parts[d]
    done[own_half, :] = total
    push(done.at[own_half], done.at[own_half], hs.at[1], hr.at[1], partner)

    second = ring_third(1, xl, 1)
    arrived(yx[1], xs.at[5], xr.at[5])
    panels[1] = second + yx[1][...]
    other_half = pl.ds(pl.multiple_of(16 * (1 - k), 16), 16)
    arrived(done.at[other_half], hs.at[1], hr.at[1])
    diagonals[0] = done[:, pl.ds(0, BS)]
    diagonals[1] = done[:, pl.ds(BS, BS)]
    at_end = jnp.where(c == 15, 1.0, 0.0).astype(F32)
    tail = pl.ds(COLS - 2 * BS, 2 * BS)
    panels[1, :, tail] = panels[1, :, tail] + at_end * done[:, pl.ds(2 * BS, 2 * BS)]
    for copy in sent:
        copy.wait_send()

    @pl.when(r == 7)
    def _():
        for d in range(7):
            remote(last, own_q, qs.at[d], qr.at[0], (d, c)).wait_send()

    @pl.when(off_diagonal)
    def _():
        for level in range(2):
            for h in range(2):
                across(level, h).wait_send()

    @pl.when(diagonal)
    def _():
        for level in range(2):
            across_chip(level).wait_send()


def local(window, pattern, row_lists, factor, diag_inverse):
    dma = pltpu.SemaphoreType.DMA
    hbm = pl.BlockSpec(memory_space=pl.ANY)
    vmem = pl.BlockSpec(memory_space=pltpu.VMEM)
    smem = pl.BlockSpec(memory_space=pltpu.SMEM)
    v = lambda *shape: pltpu.VMEM(shape, F32)
    h = lambda *shape: pltpu.VMEM(shape, BF16)
    both = lambda *shape: [v(*shape, SMALL), v(*shape, COLS)]
    panels, diagonals = pl.pallas_call(
        kernel,
        out_shape=(
            jax.ShapeDtypeStruct((2, 32, COLS), F32),
            jax.ShapeDtypeStruct((2, 32, BS), F32),
        ),
        in_specs=[vmem, smem, hbm, hbm, vmem],
        out_specs=(vmem, vmem),
        scratch_shapes=[
            v(2, 16, 16, ROWS), v(2, 8, 2, 16, COLS), v(8, 2, 16, 2 * BS), v(ROWS, COLS), h(ROWS, COLS), h(ROWS, COLS),
            h(256, ROWS), h(256, ROWS), v(2, 2, ROWS), v(2, 2, COLS), v(256, LANES), v(256, COLS),
            h(256, COLS), h(256, COLS), h(256, COLS), h(256, COLS), h(256, COLS), h(256, COLS), v(256, 256),
            v(4, 32, COLS), v(3, 32, COLS), v(32, COLS), v(32, COLS), v(16, COLS), v(16, COLS),
            both(2, 32), both(2, 32), both(2, 16), both(2, 16), both(2, 2, 32), both(32), both(32),
            v(32, SMALL), v(32, SMALL), v(8, 16, SMALL), v(32, SMALL),
            dma((2, 9)), dma((2, 9)), dma((2, 9)), dma((2, 9)), dma((2, 8)), dma((2, 8)), dma((2, 2)), dma((2, 2)),
            dma((15,)), dma((8,)), dma((1,)), dma((1,)), dma((RB // 2,)), dma((6,)),
            dma((6,)), dma((6,)), dma((5, 4)), dma((5, 4)), dma((8,)), dma((8,)), dma((2,)), dma((2,)),
        ],
        compiler_params=pltpu.CompilerParams(
            collective_id=0, has_side_effects=True, vmem_limit_bytes=63 * 1024 * 1024
        ),
        name="selected_inversion",
    )(row_lists, jnp.swapaxes(pattern, 0, 1), window, jnp.swapaxes(factor, 1, 2), diag_inverse)
    return jnp.swapaxes(panels, 1, 2), jnp.swapaxes(diagonals, 1, 2)


def solution(mesh):
    in_specs = (P("prow", "pcol"), P("prow", "pcol"), P(), P(None, "prow", "pcol"), P())
    out_specs = (P(None, "pcol", "prow"), P(None, None, "prow"))
    return jax.shard_map(local, mesh=mesh, in_specs=in_specs, out_specs=out_specs, check_vma=False)
```

time: 470 us -> 102 us (0.22); the launches traced: 465 us -> 102 us
  waiting for transfers between devices: 226 us -> 0 us
  blocking collectives: 131 us -> 0 us
  Pallas kernels: 0 us -> 98.1 us
  matrix products: 55.4 us -> 0 us
  local copies, waits for them, and re-layouts: 26.8 us -> 3.09 us
  between operations: 14.3 us -> 0.64 us
  other arithmetic: 11.4 us -> 0 us
    psum x2 -> x0, blocking collectives: 131 us -> none  [local(): gram_piece = lax.psum(product_first(owned_cols, solved), 'pcol')]
    pallas_call x0 -> x1, Pallas kernels: none -> 98.1 us  [local(): pl.pallas_call(kernel, out_shape=(jax.ShapeDtypeStruct((2, 32, COLS), F32...]
    all_gather x3 -> x0, waiting for transfers between devices: 86.9 us -> none  [the longest x2 49.6 us: local(): live_rows = lax.all_gather(live_factor, 'pcol', axis=1, tiled=True)]
    reduce_scatter x2 -> x0, waiting for transfers between devices: 70 us -> none  [local(): lax.psum_scatter(partial_value, 'prow', scatter_dimension=1, tiled=True)]
    psum x1 -> x0, waiting for transfers between devices: 68.2 us -> none  [local(): live_cols = lax.psum(mirror_rows(live_rows, local_cols), 'prow')]
    dot_general x7 -> x0, matrix products: 55.4 us -> none  [the longest x5 49.3 us: product_first(): lax.dot_general(left_side, right_side, (((0,), (0,)), ((), ())), precisio...]
    unnamed x15 -> x2, local copies, waits for them, and re-layouts: 15.3 us -> 3.09 us
    mul x5 -> x0, local copies, waits for them, and re-layouts: 9.35 us -> none  [the longest x1 9.04 us: local(): window.reshape(row_blocks, BS, col_blocks, BS) * keeper[:, None, :, None]]
  transfers between devices with their start and end apart: 6 -> 0, of which waited for: 6 -> 0; matrix products, arithmetic and copies ran while one was open for 17% -> 0% of each run, Pallas kernels for 0% -> 0%
where the time goes in v2:
time: 102 us
  Pallas kernels  98.1 us (96%)
  local copies, waits for them, and re-layouts  3.09 us (3%)
    pallas_call x1, Pallas kernels, local(): pl.pallas_call(kernel, out_shape=(jax.ShapeDtypeStruct((2, 32, COLS), F32...  98.1 us
    unnamed x2, local copies, waits for them, and re-layouts  3.09 us

profile of v2, /device:TPU:1, one launch (start us, length us, event | category | flops | bytes accessed | tf_op | source)
XLA Modules:
  0.0 101.8 jit_solution(14699032088753151200)
XLA Ops:
  0.6 98.1 %selected_inversion.1 = (f32[2,32,1280]{2,1,0:T(8,128)}, f32[2,32,128]{2,1,0:T(8,128)}) custom-call(s32[2,2,64]{2,1,0:T(2,128)} %rl_ref.1, s32[10,20]{1,0:T(8,128)} %bitcast.7, f32[2560,1280]{1,0:T(8,128)} %w_ref.1, f32[2,16,2560]{2,1,0:T(8,128)} %bitcast.4, f32[2,128,256]{2,1,0:T(8,128)} %d_ref.1), custom_call_target="tpu_custom_call" | custom-call | tf_op jit(solution)/shard_map/selected_inversion/pallas_call | solution.py:560
  98.7 1.7 %copy.9 = f32[2,1280,32]{1,2,0:T(8,128)} copy(f32[2,1280,32]{1,2,0:T(8,128)} %bitcast.5) | data formatting | bytes 655360
  100.5 1.4 %copy.10 = f32[2,128,32]{1,2,0:T(8,128)} copy(f32[2,128,32]{1,2,0:T(8,128)} %bitcast.6) | data formatting | bytes 65536

commit v3 on v2

--- a/solution.py
+++ b/solution.py
@@ -12,7 +12,7 @@
 ROWS = RB * BS
 COLS = CB * BS
 SMALL = 512
-LANES = 2 * COLS + SMALL
+CROSS = 6 * BS
 MESH = pl.DeviceIdType.MESH
 F32 = jnp.float32
 BF16 = jnp.bfloat16
@@ -45,9 +45,11 @@
     def wait(self, k, ref):
         remote(ref, ref, self.s.at[k], self.r.at[k], self.device(self.p, self.right)).wait_recv()
 
-    def start(self, src):
+    def start_pair(self, src):
+        self.push(0, src, self.block(self.p, self.y), self.device(self.q, self.y))
+
+    def start_ring(self, src):
         own = self.block(self.p, self.y)
-        self.push(0, src, own, self.device(self.q, self.y))
         self.push(1, src, own, self.device(self.p, self.right))
         self.push(2, src, own, self.device(self.p, self.left))
 
@@ -88,17 +90,19 @@
 
 
 def kernel(
-    rl_ref, pat, w_ref, f_ref, d_ref, panels, diagonals,
+    rl_ref, pat, w_ref, f_ref, d_ref, out,
     fr, fc, q_ref, w_all, wh, wl, fh, fl, mr, mc, x_ref, x1, ch, cl, c0h, c0l, ph, pw, acc,
-    ax, asum, al, ar, ahl, ahr, yl, yr, yhl, yhr, ysum, yx, fin, core, mine, parts, done,
+    ax, asum, al, ar, ahl, ahr, yin, yx, fin, bx, bsum, byin, small, core, mine, rows_in, parts, done,
     as_, ar_, bs, br, cs, cr, ts, tr, qs, qr, ks, kr, wsem, local_sem,
-    xs, xr, rs, rr, ss, sr, hs, hr,
+    xs, xr, rs, rr, ss, sr, hs, hr, gs, gr, es, er, us, ur,
 ):
     r, c, xl, y, xh, z, k = coords()
     cc = c // 2
     other = c + 1 - 2 * k
     partner = (r, other)
-    diagonal = r == cc
+    to_row = xh * 4 + (y + z) % 4
+    got = xl * 4 + (y + 4 - z) % 4
+    diagonal = jnp.logical_and(xl == xh, jnp.logical_and(y == 0, z == 0))
     off_diagonal = jnp.logical_not(diagonal)
     barrier = pltpu.get_barrier_semaphore()
 
@@ -107,8 +111,9 @@
 
     @pl.when(off_diagonal)
     def _():
-        greet((cc, 2 * r))
-        greet((cc, 2 * r + 1))
+        for h in range(2):
+            greet((to_row, 2 * r + h))
+            greet((cc, 2 * got + h))
 
     for d in range(1, 8):
         greet((r, ((cc + d) % 8) * 2 + k))
@@ -132,12 +137,10 @@
 
         return body
 
-    lax.fori_loop(0, RB, mark(mr, r * RB), 0)
-    lax.fori_loop(0, CB, mark(mc, c * CB), 0)
 
     @pl.when(off_diagonal)
     def _():
-        pl.semaphore_wait(barrier, 17)
+        pl.semaphore_wait(barrier, 19)
 
     @pl.when(diagonal)
     def _():
@@ -165,8 +168,8 @@
     def column_gather(level):
         return PairRing(
             bs.at[level], br.at[level],
-            lambda p, w: fc.at[level, p * 4 + w],
-            lambda p, w, h: fc.at[level, p * 4 + w, h],
+            lambda p, w: fc.at[level, p * 4 + (w + 4 - z) % 4],
+            lambda p, w, h: fc.at[level, p * 4 + (w + 4 - z) % 4, h],
             lambda p, w: (p * 4 + w, c),
             xl, y, sent,
         )
@@ -177,7 +180,7 @@
     def across(level, h):
         return remote(
             f_ref.at[level, :, pl.ds(h * COLS, COLS)], fc.at[level, cc, k], ts.at[level, h], tr.at[level, k],
-            (cc, 2 * r + h),
+            (to_row, 2 * r + h),
         )
 
     def across_chip(level):
@@ -188,7 +191,7 @@
 
     def across_own(level):
         return pltpu.make_async_copy(
-            f_ref.at[level, :, pl.ds(k * COLS, COLS)], fc.at[level, r, k], local_sem.at[2 + level]
+            f_ref.at[level, :, pl.ds(k * COLS, COLS)], fc.at[level, cc, k], local_sem.at[2 + level]
         )
 
     @pl.when(off_diagonal)
@@ -242,14 +245,15 @@
         @pl.when(off_diagonal)
         def _():
             for h in range(2):
-                arrived(fc.at[level, r, h], ts.at[level, h], tr.at[level, h])
+                arrived(fc.at[level, got, h], ts.at[level, h], tr.at[level, h])
 
         @pl.when(diagonal)
         def _():
-            arrived(fc.at[level, r, 1 - k], ts.at[level, 0], tr.at[level, 1 - k])
+            arrived(fc.at[level, got, 1 - k], ts.at[level, 0], tr.at[level, 1 - k])
             across_own(level).wait()
 
-        gb[level].start(fc.at[level, r])
+        gb[level].start_pair(fc.at[level, got])
+        gb[level].start_ring(fc.at[level, got])
 
     def split_window(i0, i1):
         for i in range(i0, i1):
@@ -300,65 +304,70 @@
         product(n)
         x1[:, pl.ds(n * 256, 256)] = acc[...]
 
-    ga[0].start(f_ref.at[0])
-    swap(0, cc, f_ref.at[0])
-    split_window(0, 4)
-
-    @pl.when(r == 7)
-    def _():
-        pltpu.make_async_copy(last, own_q, local_sem.at[0]).wait()
-
-    @pl.when(r != 7)
-    def _():
-        arrived(own_q, qs.at[0], qr.at[0])
-
-    for d in range(1, 8):
-        push(own_q, own_q, qs.at[7 + d], qr.at[d], (r, ((cc + d) % 8) * 2 + k))
+    def q_spread():
+        @pl.when(r == 7)
+        def _():
+            pltpu.make_async_copy(last, own_q, local_sem.at[0]).wait()
+
+        @pl.when(r != 7)
+        def _():
+            arrived(own_q, qs.at[0], qr.at[0])
+
+        for d in range(1, 8):
+            push(own_q, own_q, qs.at[7 + d], qr.at[d], (r, ((cc + d) % 8) * 2 + k))
+
+    def q_swap():
+        for d in range(1, 8):
+            arrived(q_ref.at[(cc + 8 - d) % 8, k], qs.at[0], qr.at[d])
+        half = q_ref.at[:, k]
+        push(half, half, ks.at[0], kr.at[0], partner)
+
+    def swapped(level):
+        for m in range(8):
+            arrived(fr.at[level, m * 2 + 1 - k], cs.at[level, m], cr.at[level, m])
+        own_copy[level].wait()
+
+    ga[0].start_pair(f_ref.at[0])
+    ga[0].start_ring(f_ref.at[0])
+    ga[1].start_pair(f_ref.at[1])
+    for level in range(2):
+        swap(level, cc, f_ref.at[level])
+    lax.fori_loop(0, RB, mark(mr, r * RB), 0)
     row_step(0, "left", True)
     row_step(0, "right", True)
-    ga[1].start(f_ref.at[1])
-    swap(1, cc, f_ref.at[1])
+    q_spread()
+    row_step(0, "pair", True)
+    split_window(0, 4)
     column_start(0)
     column_start(1)
-    row_step(0, "pair", True)
+    row_step(0, "far", True)
+    lax.fori_loop(0, CB, mark(mc, c * CB), 0)
+    row_step(0, "left", False)
+    row_step(0, "right", False)
+    ga[1].start_ring(f_ref.at[1])
+    row_step(1, "pair", True)
     split_window(4, 7)
+    q_swap()
     gb[0].from_left(True)
     gb[0].from_right(True)
-    row_step(0, "far", True)
+    row_step(0, "far", False)
+    split_window(7, 10)
+    gb[0].from_pair()
+    gb[1].from_pair()
+    swapped(0)
+
+    split_rows(0)
+    first_level(0)
+    gb[1].from_left(True)
+    gb[1].from_right(True)
     row_step(1, "left", True)
     row_step(1, "right", True)
-    gb[0].from_pair()
-    row_step(1, "pair", True)
-    gb[1].from_left(True)
-    gb[1].from_right(True)
-    row_step(0, "left", False)
-    row_step(0, "right", False)
-    split_window(7, 10)
-    gb[1].from_pair()
+    first_level(1)
+    first_level(2)
     gb[0].from_far(True)
-    gb[0].from_left(False)
-    gb[0].from_right(False)
     row_step(1, "far", True)
-    row_step(0, "far", False)
-    for d in range(1, 8):
-        arrived(q_ref.at[(cc + 8 - d) % 8, k], qs.at[0], qr.at[d])
-    half = q_ref.at[:, k]
-    push(half, half, ks.at[0], kr.at[0], partner)
-    for m in range(8):
-        arrived(fr.at[0, m * 2 + 1 - k], cs.at[0, m], cr.at[0, m])
-    own_copy[0].wait()
-
-    split_rows(0)
-    first_level(0)
     row_step(1, "left", False)
     row_step(1, "right", False)
-    first_level(1)
-    gb[1].from_far(True)
-    gb[1].from_left(False)
-    gb[1].from_right(False)
-    first_level(2)
-    gb[0].from_far(False)
-    row_step(1, "far", False)
     first_level(3)
     first_level(4)
 
@@ -372,42 +381,31 @@
         return pl.ds(pl.multiple_of((4 * p + w) * 32 + 16 * h, 16), 16)
 
     lane_a = pl.ds(0, COLS)
-    streams = ((2 * COLS, SMALL), (COLS, COLS))
-
-    def ring_first(t, p, v):
-        start, width = streams[t]
-        lanes = pl.ds(start, width)
-        e = 2 * t + v
-        push(x_ref.at[rows_of(p, yfar, 0), lanes], yhl[t].at[v], rs.at[e, 0], rr.at[e, 0], dr)
-        push(x_ref.at[rows_of(p, yfar, 1), lanes], yhr[t].at[v], rs.at[e, 1], rr.at[e, 1], dl)
-
-    def ring_second(t, p, v):
-        start, width = streams[t]
-        lanes = pl.ds(start, width)
-        e = 2 * t + v
-        arrived(yhl[t].at[v], rs.at[e, 0], rr.at[e, 0])
-        ysum[t][v, 0, pl.ds(0, 16), :] = x_ref[rows_of(p, yright, 0), lanes] + yhl[t][v]
-        ysum[t][v, 0, pl.ds(16, 16), :] = x_ref[rows_of(p, yright, 1), lanes]
-        push(ysum[t].at[v, 0], yl[t].at[v], rs.at[e, 2], rr.at[e, 2], dr)
-        arrived(yhr[t].at[v], rs.at[e, 1], rr.at[e, 1])
-        ysum[t][v, 1, pl.ds(0, 16), :] = x_ref[rows_of(p, yleft, 0), lanes]
-        ysum[t][v, 1, pl.ds(16, 16), :] = x_ref[rows_of(p, yleft, 1), lanes] + yhr[t][v]
-        push(ysum[t].at[v, 1], yr[t].at[v], rs.at[e, 3], rr.at[e, 3], dl)
-
-    def ring_third(t, p, v):
-        start, width = streams[t]
-        e = 2 * t + v
-        arrived(yl[t].at[v], rs.at[e, 2], rr.at[e, 2])
-        arrived(yr[t].at[v], rs.at[e, 3], rr.at[e, 3])
-        return x_ref[rows_of(p, y), pl.ds(start, width)] + (yl[t][v] + yr[t][v])
+    lane_c = pl.ds(COLS + CROSS, COLS - CROSS)
+    lane_b = pl.ds(COLS, CROSS)
+    dfar = (4 * xl + yfar, c)
+    along = ((0, yright, dr), (1, yleft, dl), (2, yfar, dfar))
+
+    def spread(p, v):
+        for i, w, device in along:
+            push(x_ref.at[rows_of(p, w), lane_c], yin.at[v, i], rs.at[v, i], rr.at[v, i], device)
+
+    def collect(p, v):
+        for i in range(3):
+            arrived(yin.at[v, i], rs.at[v, i], rr.at[v, i])
+        return (x_ref[rows_of(p, y), lane_c] + yin[v, 0]) + (yin[v, 1] + yin[v, 2])
 
     q = 1 - xl
     for w, d in ((0, yfar), (1, yright), (2, yleft), (3, y)):
         push(x_ref.at[rows_of(q, d), lane_a], ax.at[w], xs.at[w], xr.at[w], px)
 
-    for m in range(8):
-        arrived(fr.at[1, m * 2 + 1 - k], cs.at[1, m], cr.at[1, m])
-    own_copy[1].wait()
+    gb[0].from_left(False)
+    gb[0].from_right(False)
+    gb[1].from_far(True)
+    gb[1].from_left(False)
+    gb[1].from_right(False)
+    row_step(1, "far", False)
+    swapped(1)
     split_rows(1)
     second_level(0)
     arrived(ax.at[0], xs.at[0], xr.at[0])
@@ -415,7 +413,7 @@
     push(asum.at[0, pl.ds(0, 16)], ahl, rs.at[4, 0], rr.at[4, 0], dr)
     push(asum.at[0, pl.ds(16, 16)], ahr, rs.at[4, 1], rr.at[4, 1], dl)
     second_level(1)
-    gb[1].from_far(False)
+    gb[0].from_far(False)
     second_level(2)
     arrived(ax.at[1], xs.at[1], xr.at[1])
     asum[1] = x_ref[rows_of(xl, yright), lane_a] + ax[1]
@@ -430,6 +428,25 @@
     push(asum.at[2], ar, rs.at[4, 3], rr.at[4, 3], dl)
     second_level(4)
 
+    half = q_ref.at[:, 1 - k]
+    arrived(half, ks.at[0], kr.at[0])
+    qv = split(q_ref[...].reshape(256, 256))
+    ph[...], pw[...] = split(x_ref[:, lane_a])
+    def second_sum(n, carry):
+        lanes = pl.ds(pl.multiple_of(n * 256, 256), 256)
+        full = x1[:, lanes] + dot3(qv, (ph[:, lanes], pw[:, lanes]))
+        out = pl.ds(pl.multiple_of(COLS + n * 256, 256), 256)
+        for s in range(2):
+            x_ref[pl.ds(s * BS, BS), out] = -(full[s * BS:(s + 1) * BS] * mc[1, pl.ds(s, 1), lanes])
+        return carry
+
+    lax.fori_loop(0, CB // 2, second_sum, 0)
+    spread(q, 0)
+    for w, d in ((0, yfar), (1, yright), (2, yleft), (3, y)):
+        push(x_ref.at[rows_of(q, d), lane_b], bx.at[w], gs.at[w], gr.at[w], px)
+    spread(xl, 1)
+
+    gb[1].from_far(False)
     for s in range(2):
         rows = pl.ds(s * BS, BS)
 
@@ -442,10 +459,6 @@
             return carry
 
         lax.fori_loop(0, CB, body, 0)
-    half = q_ref.at[:, 1 - k]
-    arrived(half, ks.at[0], kr.at[0])
-    qv = split(q_ref[...].reshape(256, 256))
-    ph[...], pw[...] = split(x_ref[:, lane_a])
     pair = lambda h, l, rows: (h[rows, :], l[rows, :])
     whole = pl.ds(0, 256)
     a_t = dot3(pair(ch, cl, whole), pair(ph, pw, whole), nt=True)
@@ -458,7 +471,6 @@
         [dot3((qv[0][:, s * BS:(s + 1) * BS], qv[1][:, s * BS:(s + 1) * BS]), split(s_t[s])) for s in range(2)], axis=1
     )
     a_s, slot_s = split(a_t), split(slot)
-    base = 2 * COLS
     for s in range(2):
         rows = pl.ds(s * BS, BS)
         cut = lambda v: (v[0][s * BS:(s + 1) * BS], v[1][s * BS:(s + 1) * BS])
@@ -468,49 +480,43 @@
             + dot3(cut(qv), cut(a_s), nt=True)
             + dot3(cut(slot_s), cut(qv), nt=True)
         )
-        x_ref[rows, pl.ds(base, BS)] = s_t[s]
-        x_ref[rows, pl.ds(base + BS, BS)] = second
-        x_ref[rows, pl.ds(base + 2 * BS, 2 * BS)] = -slot[s * BS:(s + 1) * BS]
-    ring_first(0, q, 0)
-    ring_first(0, xl, 1)
-
-    def second_sum(n, carry):
-        lanes = pl.ds(pl.multiple_of(n * 256, 256), 256)
-        full = x1[:, lanes] + dot3(qv, (ph[:, lanes], pw[:, lanes]))
-        out = pl.ds(pl.multiple_of(COLS + n * 256, 256), 256)
-        for s in range(2):
-            x_ref[pl.ds(s * BS, BS), out] = -(full[s * BS:(s + 1) * BS] * mc[1, pl.ds(s, 1), lanes])
-        return carry
-
-    lax.fori_loop(0, CB // 2, second_sum, 0)
-    ring_first(1, q, 0)
-    ring_second(0, q, 0)
-    ring_second(0, xl, 1)
-    ring_first(1, xl, 1)
-    ring_second(1, q, 0)
-
-    fin[0][...] = ring_third(0, q, 0)
-    push(fin[0], yx[0], xs.at[4], xr.at[4], px)
-    ring_second(1, xl, 1)
-    small = ring_third(0, xl, 1)
-    arrived(yx[0], xs.at[4], xr.at[4])
-    mine[...] = small + yx[0][...]
-    push(mine, core, hs.at[0], hr.at[0], partner)
+        for lanes, value in (
+            (pl.ds(0, BS), s_t[s]), (pl.ds(BS, BS), second), (pl.ds(2 * BS, 2 * BS), -slot[s * BS:(s + 1) * BS])
+        ):
+            small[pl.ds(4 * s, 4), :, :, lanes] = value.reshape(4, 2, 16, value.shape[1])
+    theirs = small.at[:, 1 - k]
+    push(theirs, core, hs.at[0], hr.at[0], partner)
+
+    def crossed(w, i, d, device):
+        arrived(bx.at[w], gs.at[w], gr.at[w])
+        bsum[i] = x_ref[rows_of(xl, d), lane_b] + bx[w]
+        push(bsum.at[i], byin.at[i], es.at[i], er.at[i], device)
+
     arrived(core, hs.at[0], hr.at[0])
-    own_half = pl.ds(pl.multiple_of(16 * k, 16), 16)
-    parts[cc] = mine[own_half, :] + core[own_half, :]
+    mine[...] = small[:, k] + core[...]
+    for d in range(1, 8):
+        to = (r + d) % 8
+        push(mine.at[to], rows_in.at[d - 1], us.at[d], ur.at[d], (to, c))
+    crossed(0, 2, yfar, dfar)
+    crossed(1, 0, yright, dr)
+    crossed(2, 1, yleft, dl)
+    total = mine[r]
+    for d in range(1, 8):
+        arrived(rows_in.at[d - 1], us.at[d], ur.at[d])
+        total = total + rows_in[d - 1]
+    parts[cc] = total
     for d in range(1, 8):
         push(parts.at[cc], parts.at[cc], ss.at[d], sr.at[d], (r, ((cc + d) % 8) * 2 + k))
-
-    fin[1][...] = ring_third(1, q, 0)
-    push(fin[1], yx[1], xs.at[5], xr.at[5], px)
+    fin[...] = collect(q, 0)
+    push(fin, yx, xs.at[5], xr.at[5], px)
 
     arrived(ax.at[3], xs.at[3], xr.at[3])
     first = x_ref[rows_of(xl, y), lane_a] + ax[3]
     arrived(al, rs.at[4, 2], rr.at[4, 2])
     arrived(ar, rs.at[4, 3], rr.at[4, 3])
-    panels[0] = first + (al[...] + ar[...])
-
+    out[0, :, lane_a] = first + (al[...] + ar[...])
+
+    own_half = pl.ds(pl.multiple_of(16 * k, 16), 16)
     for d in range(1, 8):
         arrived(parts.at[(cc + 8 - d) % 8], ss.at[d], sr.at[d])
     total = parts[0]
@@ -519,16 +525,23 @@
     done[own_half, :] = total
     push(done.at[own_half], done.at[own_half], hs.at[1], hr.at[1], partner)
 
-    second = ring_third(1, xl, 1)
-    arrived(yx[1], xs.at[5], xr.at[5])
-    panels[1] = second + yx[1][...]
+    lane_d = pl.ds(CROSS, COLS - CROSS)
+    lane_e = pl.ds(COLS, BS)
+    out[1, :, lane_d] = collect(xl, 1)
+    arrived(bx.at[3], gs.at[3], gr.at[3])
+    second = x_ref[rows_of(xl, y), lane_b] + bx[3]
+    arrived(yx, xs.at[5], xr.at[5])
+    out[1, :, lane_d] = out[1, :, lane_d] + yx[...]
+    for i in range(3):
+        arrived(byin.at[i], es.at[i], er.at[i])
+    out[1, :, pl.ds(0, CROSS)] = (second + byin[0]) + (byin[1] + byin[2])
     other_half = pl.ds(pl.multiple_of(16 * (1 - k), 16), 16)
     arrived(done.at[other_half], hs.at[1], hr.at[1])
-    diagonals[0] = done[:, pl.ds(0, BS)]
-    diagonals[1] = done[:, pl.ds(BS, BS)]
+    out[0, :, lane_e] = done[:, pl.ds(0, BS)]
+    out[1, :, lane_e] = done[:, pl.ds(BS, BS)]
     at_end = jnp.where(c == 15, 1.0, 0.0).astype(F32)
     tail = pl.ds(COLS - 2 * BS, 2 * BS)
-    panels[1, :, tail] = panels[1, :, tail] + at_end * done[:, pl.ds(2 * BS, 2 * BS)]
+    out[1, :, tail] = out[1, :, tail] + at_end * done[:, pl.ds(2 * BS, 2 * BS)]
     for copy in sent:
         copy.wait_send()
 
@@ -556,32 +569,29 @@
     smem = pl.BlockSpec(memory_space=pltpu.SMEM)
     v = lambda *shape: pltpu.VMEM(shape, F32)
     h = lambda *shape: pltpu.VMEM(shape, BF16)
-    both = lambda *shape: [v(*shape, SMALL), v(*shape, COLS)]
-    panels, diagonals = pl.pallas_call(
+    both_levels = pl.pallas_call(
         kernel,
-        out_shape=(
-            jax.ShapeDtypeStruct((2, 32, COLS), F32),
-            jax.ShapeDtypeStruct((2, 32, BS), F32),
-        ),
+        out_shape=jax.ShapeDtypeStruct((2, 32, COLS + BS), F32),
         in_specs=[vmem, smem, hbm, hbm, vmem],
-        out_specs=(vmem, vmem),
+        out_specs=vmem,
         scratch_shapes=[
             v(2, 16, 16, ROWS), v(2, 8, 2, 16, COLS), v(8, 2, 16, 2 * BS), v(ROWS, COLS), h(ROWS, COLS), h(ROWS, COLS),
-            h(256, ROWS), h(256, ROWS), v(2, 2, ROWS), v(2, 2, COLS), v(256, LANES), v(256, COLS),
+            h(256, ROWS), h(256, ROWS), v(2, 2, ROWS), v(2, 2, COLS), v(256, 2 * COLS), v(256, COLS),
             h(256, COLS), h(256, COLS), h(256, COLS), h(256, COLS), h(256, COLS), h(256, COLS), v(256, 256),
             v(4, 32, COLS), v(3, 32, COLS), v(32, COLS), v(32, COLS), v(16, COLS), v(16, COLS),
-            both(2, 32), both(2, 32), both(2, 16), both(2, 16), both(2, 2, 32), both(32), both(32),
-            v(32, SMALL), v(32, SMALL), v(8, 16, SMALL), v(32, SMALL),
+            v(2, 3, 32, COLS - CROSS), v(32, COLS - CROSS), v(32, COLS - CROSS), v(4, 32, CROSS), v(3, 32, CROSS), v(3, 32, CROSS),
+            v(8, 2, 16, SMALL), v(8, 16, SMALL), v(8, 16, SMALL), v(7, 16, SMALL), v(8, 16, SMALL), v(32, SMALL),
             dma((2, 9)), dma((2, 9)), dma((2, 9)), dma((2, 9)), dma((2, 8)), dma((2, 8)), dma((2, 2)), dma((2, 2)),
             dma((15,)), dma((8,)), dma((1,)), dma((1,)), dma((RB // 2,)), dma((6,)),
             dma((6,)), dma((6,)), dma((5, 4)), dma((5, 4)), dma((8,)), dma((8,)), dma((2,)), dma((2,)),
+            dma((4,)), dma((4,)), dma((3,)), dma((3,)), dma((8,)), dma((8,)),
         ],
         compiler_params=pltpu.CompilerParams(
             collective_id=0, has_side_effects=True, vmem_limit_bytes=63 * 1024 * 1024
         ),
         name="selected_inversion",
     )(row_lists, jnp.swapaxes(pattern, 0, 1), window, jnp.swapaxes(factor, 1, 2), diag_inverse)
-    return jnp.swapaxes(panels, 1, 2), jnp.swapaxes(diagonals, 1, 2)
+    return jnp.swapaxes(both_levels[:, :, :COLS], 1, 2), jnp.swapaxes(both_levels[:, :, COLS:], 1, 2)
 
 
 def solution(mesh):

time: 102 us -> 89.8 us (0.88)
  Pallas kernels: 98.1 us -> 85.8 us
    pallas_call x1, Pallas kernels: 98.1 us -> 85.8 us  [local(): pl.pallas_call(kernel, out_shape=jax.ShapeDtypeStruct((2, 32, COLS + BS),...]
    transpose x0 -> x2, local copies, waits for them, and re-layouts: none -> 3.09 us  [the longest x1 1.72 us: local(): jnp.swapaxes(both_levels[:, :, :COLS], 1, 2)]
    unnamed x2 -> x0, local copies, waits for them, and re-layouts: 3.09 us -> none
where the time goes in v3:
time: 89.8 us; the launch traced here: 89.5 us
  Pallas kernels  85.8 us (96%)
  local copies, waits for them, and re-layouts  3.09 us (3%)
    pallas_call x1, Pallas kernels, local(): pl.pallas_call(kernel, out_shape=jax.ShapeDtypeStruct((2, 32, COLS + BS),...  85.8 us

profile of v3, /device:TPU:1, one launch (start us, length us, event | category | flops | bytes accessed | tf_op | source)
XLA Modules:
  0.0 89.5 jit_solution(11753385590327195274)
XLA Ops:
  0.6 85.8 %selected_inversion.1 = f32[2,32,1408]{2,1,0:T(8,128)} custom-call(s32[2,2,64]{2,1,0:T(2,128)} %rl_ref.1, s32[10,20]{1,0:T(8,128)} %bitcast.7, f32[2560,1280]{1,0:T(8,128)} %w_ref.1, f32[2,16,2560]{2,1,0:T(8,128)} %bitcast.6, f32[2,128,256]{2,1,0:T(8,128)} %d_ref.1), custom_call_target="tpu_custom_call" | custom-call | tf_op jit(solution)/shard_map/selected_inversion/pallas_call | solution.py:572
  86.5 1.4 %slice_bitcast_fusion.1 = f32[2,128,32]{1,2,0:T(8,128)} fusion(f32[2,32,1408]{2,1,0:T(8,128)} %selected_inversion.1), kind=kLoop, calls=%fused_computation.1 | loop fusion | bytes 65536 | tf_op jit(solution)/shard_map/transpose | solution.py:594
  87.8 1.7 %slice_bitcast_fusion = f32[2,1280,32]{1,2,0:T(8,128)} fusion(f32[2,32,1408]{2,1,0:T(8,128)} %selected_inversion.1), kind=kLoop, calls=%fused_computation | loop fusion | bytes 655360 | tf_op jit(solution)/shard_map/transpose | solution.py:594

commit v4 on v3

--- a/solution.py
+++ b/solution.py
@@ -287,11 +287,11 @@
         lanes = pl.ds(n * 256, 256)
 
         def body(i, carry):
-            depth = pl.ds(pl.multiple_of(i * 512, 512), 512)
+            depth = pl.ds(pl.multiple_of(i * 1280, 1280), 1280)
             acc[...] += dot3((fh[:, depth], fl[:, depth]), (wh[depth, lanes], wl[depth, lanes]))
             return carry
 
-        lax.fori_loop(0, RB // 4, body, 0)
+        lax.fori_loop(0, ROWS // 1280, body, 0)
 
     def first_level(n):
         product(n)
@@ -560,6 +560,11 @@
     def _():
         for level in range(2):
             across_chip(level).wait_send()
+
+
+def part_kernel(both_ref, panels, diagonals):
+    panels[...] = both_ref[:, :, pl.ds(0, COLS)]
+    diagonals[...] = both_ref[:, :, pl.ds(COLS, BS)]
 
 
 def local(window, pattern, row_lists, factor, diag_inverse):
@@ -591,7 +596,14 @@
         ),
         name="selected_inversion",
     )(row_lists, jnp.swapaxes(pattern, 0, 1), window, jnp.swapaxes(factor, 1, 2), diag_inverse)
-    return jnp.swapaxes(both_levels[:, :, :COLS], 1, 2), jnp.swapaxes(both_levels[:, :, COLS:], 1, 2)
+    panels, diagonals = pl.pallas_call(
+        part_kernel,
+        out_shape=(jax.ShapeDtypeStruct((2, 32, COLS), F32), jax.ShapeDtypeStruct((2, 32, BS), F32)),
+        in_specs=[vmem],
+        out_specs=(vmem, vmem),
+        name="parts",
+    )(both_levels)
+    return jnp.swapaxes(panels, 1, 2), jnp.swapaxes(diagonals, 1, 2)
 
 
 def solution(mesh):

time: 89.8 us -> 85.6 us (0.953)
  local copies, waits for them, and re-layouts: 3.09 us -> 0 us
  Pallas kernels: 85.8 us -> 84.8 us
    transpose x2 -> x0, local copies, waits for them, and re-layouts: 3.09 us -> none  [the longest x1 1.72 us: local(): jnp.swapaxes(both_levels[:, :, :COLS], 1, 2)]
    pallas_call x1, Pallas kernels: 85.8 us -> 83.1 us  [local(): pl.pallas_call(kernel, out_shape=jax.ShapeDtypeStruct((2, 32, COLS + BS),...]
    pallas_call x0 -> x1, Pallas kernels: none -> 1.73 us  [local(): pl.pallas_call(part_kernel, out_shape=(jax.ShapeDtypeStruct((2, 32, COLS)...]
where the time goes in v4:
time: 85.6 us; the launch traced here: 85.4 us
  Pallas kernels  84.8 us (99%)
    pallas_call x1, Pallas kernels, local(): pl.pallas_call(kernel, out_shape=jax.ShapeDtypeStruct((2, 32, COLS + BS),...  83.1 us
    pallas_call x1, Pallas kernels, local(): pl.pallas_call(part_kernel, out_shape=(jax.ShapeDtypeStruct((2, 32, COLS)...  1.73 us

profile of v4, /device:TPU:1, one launch (start us, length us, event | category | flops | bytes accessed | tf_op | source)
XLA Modules:
  0.0 85.4 jit_solution(14717348288899113743)
XLA Ops:
  0.6 83.1 %selected_inversion.1.both_ref = f32[2,32,1408]{2,1,0:T(8,128)} custom-call(s32[2,2,64]{2,1,0:T(2,128)} %rl_ref.1, s32[10,20]{1,0:T(8,128)} %bitcast.5, f32[2560,1280]{1,0:T(8,128)} %w_ref.1, f32[2,16,2560]{2,1,0:T(8,128)} %bitcast.4, f32[2,128,256]{2,1,0:T(8,128)} %d_ref.1), custom_call_target="tpu_custom_call" | custom-call | tf_op jit(solution)/shard_map/selected_inversion/pallas_call | solution.py:577
  83.7 1.7 %parts.1 = (f32[2,32,1280]{2,1,0:T(8,128)}, f32[2,32,128]{2,1,0:T(8,128)}) custom-call(f32[2,32,1408]{2,1,0:T(8,128)} %selected_inversion.1.both_ref), custom_call_target="tpu_custom_call" | custom-call | tf_op jit(solution)/shard_map/parts/pallas_call | solution.py:599

commit v5 on v4

--- a/solution.py
+++ b/solution.py
@@ -396,14 +396,14 @@
         return (x_ref[rows_of(p, y), lane_c] + yin[v, 0]) + (yin[v, 1] + yin[v, 2])
 
     q = 1 - xl
-    for w, d in ((0, yfar), (1, yright), (2, yleft), (3, y)):
-        push(x_ref.at[rows_of(q, d), lane_a], ax.at[w], xs.at[w], xr.at[w], px)
 
     gb[0].from_left(False)
     gb[0].from_right(False)
     gb[1].from_far(True)
     gb[1].from_left(False)
     gb[1].from_right(False)
+    for w, d in ((0, yfar), (1, yright), (2, yleft), (3, y)):
+        push(x_ref.at[rows_of(q, d), lane_a], ax.at[w], xs.at[w], xr.at[w], px)
     row_step(1, "far", False)
     swapped(1)
     split_rows(1)

time: 85.6 us -> 85.8 us (level)
  no operation moved by 1% of the time
where the time goes in v5:
time: 85.8 us; the launch traced here: 85.6 us
  Pallas kernels  85 us (99%)
    pallas_call x1, Pallas kernels, local(): pl.pallas_call(kernel, out_shape=jax.ShapeDtypeStruct((2, 32, COLS + BS),...  83.2 us
    pallas_call x1, Pallas kernels, local(): pl.pallas_call(part_kernel, out_shape=(jax.ShapeDtypeStruct((2, 32, COLS)...  1.73 us

profile of v5, /device:TPU:1, one launch (start us, length us, event | category | flops | bytes accessed | tf_op | source)
XLA Modules:
  0.0 85.6 jit_solution(7345443765968992479)
XLA Ops:
  0.6 83.2 %selected_inversion.1.both_ref = f32[2,32,1408]{2,1,0:T(8,128)} custom-call(s32[2,2,64]{2,1,0:T(2,128)} %rl_ref.1, s32[10,20]{1,0:T(8,128)} %bitcast.5, f32[2560,1280]{1,0:T(8,128)} %w_ref.1, f32[2,16,2560]{2,1,0:T(8,128)} %bitcast.4, f32[2,128,256]{2,1,0:T(8,128)} %d_ref.1), custom_call_target="tpu_custom_call" | custom-call | tf_op jit(solution)/shard_map/selected_inversion/pallas_call | solution.py:577
  83.9 1.7 %parts.1 = (f32[2,32,1280]{2,1,0:T(8,128)}, f32[2,32,128]{2,1,0:T(8,128)}) custom-call(f32[2,32,1408]{2,1,0:T(8,128)} %selected_inversion.1.both_ref), custom_call_target="tpu_custom_call" | custom-call | tf_op jit(solution)/shard_map/parts/pallas_call | solution.py:599
